TPU v7x, 512 devices: a whole 4x8x8 slice. The times are simulated.
512 devices in a mesh: vol: 128 (over y, z, core), rep: 4 (over x).
Axes of the slice: x: 4, y: 8, z: 8, core: 2. Of those that a mesh axis runs over, the one named last changes fastest.
Arguments:
- surface_state: float32 [14336, 32, 128], P('vol', 'rep'), may hold values from -6 to 6
- direction: float32 [14336, 32, 128], P('vol', 'rep'), may hold values from -6 to 6
- stiffness: float32 [14336, 128], P('vol'), may hold values from 0.5 to 5
- partners: int32 [14336, 4], P('vol'), may hold values from 0 to 14335, as said below
- contact_owner: int32 [14336], P('vol'), may hold values from 0 to 127, as said below
- projection: float32 [32, 32], replicated, may hold values from -1 to 1
- mortar: float32 [4, 128, 128], replicated, may hold values from -0.5 to 0.5
Outputs:
- hessian_product: float32 [14336, 32, 128], P('vol', 'rep')
Inputs may be any that keep to these rules, and one draw needn't show every extreme that they name: `contact_owner`: in the 112 blocks of one volume owner (aligned blocks of rows) no contact owner is named more than 2 times; 14 contact owners are named exactly 2 times in every such block. `partners`: partners may repeat, may be the block itself, and may have another contact owner than their block.
All inputs are finite; a program needn't handle non-finite values.
Results may differ from a plain program's by a relative error of at most 0.0001.
Values sent between devices are 32-bit elements; how exact they have to be, the bound alone decides.
A program may use at most 64 MiB of HBM per device.

v0:
```python
import jax
import jax.numpy as jnp
from jax import lax
from jax.sharding import PartitionSpec as P

sharpness = 1.5


def local(surface_state, direction, stiffness, partners, contact_owner, projection, mortar):
    highest = lax.Precision.HIGHEST
    vol_count = lax.axis_size("vol")
    rep_index = lax.axis_index("rep")
    vol_index = lax.axis_index("vol")
    blocks, channel_share, face_count = surface_state.shape
    partner_count = partners.shape[1]
    capacity = max(2, (2 * blocks + vol_count - 1) // vol_count)
    slot_count = vol_count * capacity
    my_columns = lax.dynamic_slice_in_dim(projection, rep_index * channel_share, channel_share, 1)
    my_rows = lax.dynamic_slice_in_dim(projection, rep_index * channel_share, channel_share, 0)

    def fold_one(piece):
        return jnp.einsum("ij,bjf->bif", my_rows, piece, precision=highest)

    counter = jnp.arange(blocks, dtype=jnp.int32)
    same_owner = contact_owner[:, None] == contact_owner[None, :]
    earlier = counter[:, None] < counter[None, :]
    bucket_rank = jnp.sum((same_owner & earlier).astype(jnp.int32), axis=0)
    slot_of = contact_owner * capacity + bucket_rank
    slot_iota = jnp.arange(slot_count, dtype=jnp.int32)
    matches = slot_iota[:, None] == slot_of[None, :]
    occupied = jnp.any(matches, axis=1).astype(jnp.float32)
    source_row = jnp.sum(jnp.where(matches, counter[None, :], 0), axis=1)
    global_ids = vol_index * blocks + counter
    labels = jnp.concatenate([(global_ids + 1)[:, None], partners], axis=1).astype(jnp.float32)
    send_stiff = (stiffness[source_row] * occupied[:, None]).reshape(
        vol_count, capacity, face_count
    )
    send_labels = (labels[source_row] * occupied[:, None]).reshape(
        vol_count, capacity, partner_count + 1
    )

    def pack(values):
        return (values[source_row] * occupied[:, None, None]).reshape(
            vol_count, capacity, channel_share, face_count
        )

    projected = fold_one(lax.all_gather(surface_state, "rep", axis=1, tiled=True))
    moving = fold_one(lax.all_gather(direction, "rep", axis=1, tiled=True))
    received = (
        lax.all_to_all(pack(projected), "vol", split_axis=0, concat_axis=0, tiled=True),
        lax.all_to_all(pack(moving), "vol", split_axis=0, concat_axis=0, tiled=True),
        lax.all_to_all(send_stiff, "vol", split_axis=0, concat_axis=0, tiled=True),
        lax.all_to_all(send_labels, "vol", split_axis=0, concat_axis=0, tiled=True),
    )
    got_state = received[0].reshape(slot_count, channel_share, face_count)
    got_move = received[1].reshape(slot_count, channel_share, face_count)
    got_stiff = received[2].reshape(slot_count, face_count)
    got_labels = received[3].reshape(slot_count, partner_count + 1).astype(jnp.int32)
    slot_ids = got_labels[:, 0] - 1
    partner_ids = got_labels[:, 1:]
    partner_source = partner_ids // blocks
    candidates = slot_ids.reshape(vol_count, capacity)[partner_source]
    offsets = jnp.arange(capacity, dtype=jnp.int32)
    matched = candidates == partner_ids[..., None]
    found = jnp.any(matched, axis=2).astype(jnp.float32)
    partner_offset = jnp.sum(jnp.where(matched, offsets, 0), axis=2)
    partner_slot = partner_source * capacity + partner_offset
    mapped_state = jnp.einsum("rcf,kfg->krcg", got_state, mortar, precision=highest)
    weights = []
    for column in range(partner_count):
        target = partner_slot[:, column]
        contact_gap = got_state - mapped_state[column][target]
        squashed = jax.nn.sigmoid(sharpness * contact_gap)
        weights.append(
            found[:, column][:, None, None]
            * got_stiff[:, None, :]
            * sharpness
            * squashed
            * (1.0 - squashed)
        )
    partner_slot, weights = (partner_slot, weights)
    mapped_move = jnp.einsum("rcf,kfg->krcg", got_move, mortar, precision=highest)
    tangent = jnp.zeros_like(got_move)
    returns = []
    for column in range(partner_count):
        target = partner_slot[:, column]
        traction = weights[column] * (got_move - mapped_move[column][target])
        tangent = tangent + traction
        returns.append(jax.ops.segment_sum(traction, target, num_segments=slot_count))
    returned = jnp.einsum("krcg,kfg->rcf", jnp.stack(returns), mortar, precision=highest)
    summed = (tangent - returned).reshape(vol_count, capacity, channel_share, face_count)
    returned_tiles = lax.all_to_all(summed, "vol", split_axis=0, concat_axis=0, tiled=True)
    own_tangent = returned_tiles.reshape(slot_count, channel_share, face_count)[slot_of]
    return jnp.einsum(
        "ji,bjf->bif",
        my_columns,
        lax.all_gather(own_tangent, "rep", axis=1, tiled=True),
        precision=highest,
    )


def solution(mesh):
    placed = (
        P("vol", "rep", None),
        P("vol", "rep", None),
        P("vol", None),
        P("vol", None),
        P("vol"),
        P(),
        P(),
    )
    return jax.shard_map(
        local, mesh=mesh, in_specs=placed, out_specs=P("vol", "rep", None), check_vma=False
    )
```

profile of v0, /device:TPU:1, one launch (start us, length us, event | category | flops | bytes accessed | tf_op | source)
XLA Modules:
  0.0 432.5 jit_solution(17351768416269930286)
XLA Ops:
  13.1 18.4 %all-to-all-start = ((f32[128,2,5]{2,1,0:T(2,128)}), f32[128,2,5]{2,1,0:T(2,128)S(1)}, u32[]{:S(2)}, u32[]{:S(2)}) async-start(f32[128,2,5]{2,1,0:T(2,128)} %broadcast_multiply_fusion.3), calls=%async_computation | async-start | bytes 262144 | tf_op jit(solution)/shard_map/all_to_all | solution.py:53
  31.5 1.5 gather_fusion.2
  33.9 17.9 %all-gather.7.cloned.1.call-done = f32[112,32,128]{2,1,0:T(8,128)} async-done(((f32[112,8,128]{2,1,0:T(8,128)}), f32[112,32,128]{2,1,0:T(8,128)}) %all-gather.7.cloned.1.call-update) | async-done | bytes 1835024 | tf_op jit(solution)/shard_map/all_gather | solution.py:48
  51.8 2.5 convolution_bitcast_fusion.3
  54.3 38.3 %all-gather.5.cloned.1.call-done = f32[112,32,128]{2,1,0:T(8,128)} async-done(((f32[112,8,128]{2,1,0:T(8,128)}), f32[112,32,128]{2,1,0:T(8,128)}) %all-gather.5.cloned.1.call-update) | async-done | bytes 1835024 | tf_op jit(solution)/shard_map/all_gather | solution.py:47
  92.6 2.5 convolution_bitcast_fusion.4
  97.8 15.2 %all-to-all-start.1 = ((f32[128,2,128]{2,1,0:T(2,128)}), f32[128,2,128]{2,1,0:T(2,128)S(1)}, u32[]{:S(2)}, u32[]{:S(2)}) async-start(f32[128,2,128]{2,1,0:T(2,128)} %broadcast_multiply_fusion.2), calls=%async_computation.1 | async-start | bytes 262144 | tf_op jit(solution)/shard_map/all_to_all | solution.py:52
  113.0 1.7 broadcast_multiply_fusion.1
  114.7 10.4 %all-to-all-done.1 = f32[128,2,128]{2,1,0:T(2,128)S(1)} async-done(((f32[128,2,128]{2,1,0:T(2,128)}), f32[128,2,128]{2,1,0:T(2,128)S(1)}, u32[]{:S(2)}, u32[]{:S(2)}) %all-to-all-start.1) | async-done | bytes 131104 | tf_op jit(solution)/shard_map/all_to_all | solution.py:52
  125.1 6.3 %all-to-all-start.3 = ((f32[128,2,8,128]{3,2,1,0:T(8,128)}), f32[128,2,8,128]{3,2,1,0:T(8,128)S(1)}, u32[]{:S(2)}, u32[]{:S(2)}) async-start(f32[128,2,8,128]{3,2,1,0:T(8,128)} %get-tuple-element.40), calls=%async_computation.3 | async-start | bytes 2097152 | tf_op jit(solution)/shard_map/all_to_all | solution.py:51
  131.8 30.0 %all-to-all-done.3 = f32[128,2,8,128]{3,2,1,0:T(8,128)S(1)} async-done(((f32[128,2,8,128]{3,2,1,0:T(8,128)}), f32[128,2,8,128]{3,2,1,0:T(8,128)S(1)}, u32[]{:S(2)}, u32[]{:S(2)}) %all-to-all-start.3) | async-done | bytes 1048608 | tf_op jit(solution)/shard_map/all_to_all | solution.py:51
  161.8 17.9 %all-to-all-start.2 = ((f32[128,2,8,128]{3,2,1,0:T(8,128)}), f32[128,2,8,128]{3,2,1,0:T(8,128)S(1)}, u32[]{:S(2)}, u32[]{:S(2)}) async-start(f32[128,2,8,128]{3,2,1,0:T(8,128)} %get-tuple-element.39), calls=%async_computation.2 | async-start | bytes 2097152 | tf_op jit(solution)/shard_map/all_to_all | solution.py:50
  179.9 2.8 gather_fusion.1
  182.8 4.8 %fusion.60 = (pred[256,4]{1,0:T(8,128)(4,1)S(1)}, pred[256,4,2]{2,1,0:T(4,128)(4,1)S(1)}) fusion(s32[256,4,2]{2,1,0:T(4,128)S(1)} %bitcast.96, s32[256,4]{1,0:T(8,128)S(1)} %get-tuple-element.37), kind=kLoop, calls=%fused_computation.143 | loop fusion | flops 3072 | bytes 15360 | tf_op jit(solution)/shard_map/reduce_or | solution.py:65
  187.6 4.4 %select_reduce_fusion = s32[256,4]{1,0:T(8,128)S(1)} fusion(pred[256,4,2]{2,1,0:T(4,128)(4,1)S(1)} %get-tuple-element.20), kind=kLoop, calls=%fused_computation.77 | loop fusion | flops 3072 | bytes 6144 | tf_op jit(solution)/shard_map/reduce_sum | solution.py:66
  196.3 3.4 convolution_bitcast_fusion
  199.8 1.7 slice_bitcast_fusion.6
  202.1 8.0 %all-to-all-done.2 = f32[128,2,8,128]{3,2,1,0:T(8,128)S(1)} async-done(((f32[128,2,8,128]{3,2,1,0:T(8,128)}), f32[128,2,8,128]{3,2,1,0:T(8,128)S(1)}, u32[]{:S(2)}, u32[]{:S(2)}) %all-to-all-start.2) | async-done | bytes 1048608 | tf_op jit(solution)/shard_map/all_to_all | solution.py:50
  210.6 3.9 convolution_bitcast_fusion.1
  214.5 1.7 slice_bitcast_fusion.7
  216.2 1.6 copy.131
  218.4 3.0 gather_fusion.11
  221.5 2.0 gather_fusion.12
  223.5 1.9 copy.118
  225.4 2.8 copy.123
  228.2 1.7 copy.125
  229.9 3.0 gather_fusion.7
  232.9 3.0 gather_fusion.8
  235.9 2.8 copy.127
  238.7 2.1 gather_fusion.10
  240.8 3.2 gather_fusion.9
  244.0 1.8 copy.121
  245.9 2.1 gather_fusion.4
  248.0 2.1 gather_fusion.6
  250.1 6.7 %fusion.32 = (f32[256,8,128]{2,0,1:T(8,128)S(1)}, f32[256,8,128]{2,0,1:T(8,128)S(1)}, f32[256,8,128]{2,0,1:T(8,128)}, f32[256,8,128]{2,0,1:T(8,128)}) fusion(f32[256,8,128]{2,0,1:T(8,128)S(1)} %bitcast.85, f32[256,8,128]{2,1,0:T(8,128)} %gather_fusion.6, f32[256,8,128]{2,0,1:T(8,128)} %bitcast.87, f32[256,8,128]{2,1,0:T(8,128)} %gather_fusion.4, ...), kind=kLoop, calls=%fused_computation.70 | loop fusion | flops 10485760 | bytes 15204352 | tf_op jit(solution)/shard_map/mul | solution.py:87
  256.9 1.6 copy.139
  258.5 18.9 %scatter_fusion.2 = f32[256,8,128]{2,1,0:T(8,128)S(1)} fusion(f32[256,8,128]{2,1,0:T(8,128)S(1)} %broadcast.140.clone.1, s32[256]{0:T(256)} %get-tuple-element.14, f32[256,8,128]{2,1,0:T(8,128)} %copy.139), kind=kCustom, calls=%fused_computation.16 | custom fusion | flops 262144 | bytes 3146752 | tf_op jit(solution)/shard_map/scatter-add | solution.py:89
  278.6 2.9 copy.137
  281.6 18.6 %scatter_fusion.1 = f32[256,8,128]{2,1,0:T(8,128)S(1)} fusion(f32[256,8,128]{2,1,0:T(8,128)S(1)} %broadcast.140.clone.2, s32[256]{0:T(256)S(1)} %copy-done.12, f32[256,8,128]{2,1,0:T(8,128)} %copy.137), kind=kCustom, calls=%fused_computation.15 | custom fusion | flops 262144 | bytes 3146752 | tf_op jit(solution)/shard_map/scatter-add | solution.py:89
  301.4 1.6 copy.135
  303.1 18.6 %scatter_fusion = f32[256,8,128]{2,1,0:T(8,128)S(1)} fusion(f32[256,8,128]{2,1,0:T(8,128)S(1)} %broadcast.140.clone.3, s32[256]{0:T(256)S(1)} %copy-done.11, f32[256,8,128]{2,1,0:T(8,128)} %copy.135), kind=kCustom, calls=%fused_computation.14 | custom fusion | flops 262144 | bytes 3146752 | tf_op jit(solution)/shard_map/scatter-add | solution.py:89
  322.8 2.9 copy.141
  325.8 18.6 %scatter_fusion.3 = f32[256,8,128]{2,1,0:T(8,128)S(1)} fusion(f32[256,8,128]{2,1,0:T(8,128)S(1)} %broadcast.140.clone, s32[256]{0:T(256)S(1)} %copy-done.10, f32[256,8,128]{2,1,0:T(8,128)} %copy.141), kind=kCustom, calls=%fused_computation.17 | custom fusion | flops 262144 | bytes 3146752 | tf_op jit(solution)/shard_map/scatter-add | solution.py:89
  344.6 6.1 %fusion.11 = f32[256,8,128]{2,0,1:T(8,128)S(1)} fusion(f32[1,256,8,128]{3,1,0,2:T(8,128)S(1)} %bitcast.91, f32[1,256,8,128]{3,1,0,2:T(8,128)} %bitcast.88, f32[1,256,8,128]{3,1,0,2:T(8,128)} %bitcast.89, f32[1,256,8,128]{3,1,0,2:T(8,128)} %bitcast.90, f32[256,8,128]{2,0,1:T(8,128)} %get-tuple-element.32, f32[256,8,128]{2,0,1:T(8,128)S(1)} %get-tuple-element.30, ...), kind=kOutput, calls=%fused_computation.29 | convolution fusion | flops 1614807040 | bytes 9699328 | tf_op jit(solution)/shard_map/krcg,kfg->rcf/dot_general | solution.py:90
  352.0 7.7 %all-to-all-start.4 = ((f32[128,2,8,128]{3,1,2,0:T(2,128)}), f32[128,2,8,128]{3,1,2,0:T(2,128)S(1)}, u32[]{:S(2)}, u32[]{:S(2)}) async-start(f32[128,2,8,128]{3,1,2,0:T(2,128)} %copy.143), calls=%async_computation.4 | async-start | bytes 2097152 | tf_op jit(solution)/shard_map/all_to_all | solution.py:92
  359.8 30.4 %all-to-all-done.4 = f32[128,2,8,128]{3,1,2,0:T(2,128)S(1)} async-done(((f32[128,2,8,128]{3,1,2,0:T(2,128)}), f32[128,2,8,128]{3,1,2,0:T(2,128)S(1)}, u32[]{:S(2)}, u32[]{:S(2)}) %all-to-all-start.4) | async-done | bytes 1048608 | tf_op jit(solution)/shard_map/all_to_all | solution.py:92
  391.8 30.6 %all-gather.9.cloned.1.call-done = f32[112,32,128]{2,1,0:T(8,128)} async-done(((f32[112,8,128]{2,1,0:T(8,128)}), f32[112,32,128]{2,1,0:T(8,128)}) %all-gather.9.cloned.1.call-update) | async-done | bytes 1835024 | tf_op jit(solution)/shard_map/all_gather | solution.py:97
  422.4 3.4 convolution_bitcast_fusion.2
  (81 shorter events, 23.8 us)
Async XLA Ops:
  6.5 189.8 %copy-start = (f32[4,128,128]{2,1,0:T(8,128)S(1)}, f32[4,128,128]{2,1,0:T(8,128)}, u32[]{:S(2)}) copy-start(f32[4,128,128]{2,1,0:T(8,128)} %param.13) | copy-start | bytes 786436
  6.5 45.2 %copy-start.7 = (f32[32,32]{1,0:T(8,128)S(1)}, f32[32,32]{1,0:T(8,128)}, u32[]{:S(2)}) copy-start(f32[32,32]{1,0:T(8,128)} %param.12) | copy-start | bytes 12292
  6.5 45.2 %all-gather.7.cloned.1.call-start = ((), (), s32[]{:S(2)}) async-start(), calls=%async_computation.6 | async-start | bytes 2293760 | tf_op jit(solution)/shard_map/all_gather | solution.py:48
  7.3 85.3 %all-gather.5.cloned.1.call-start = ((), (), s32[]{:S(2)}) async-start(), calls=%async_computation.5 | async-start | bytes 2293760 | tf_op jit(solution)/shard_map/all_gather | solution.py:47
  13.1 84.1 %all-to-all-start = ((f32[128,2,5]{2,1,0:T(2,128)}), f32[128,2,5]{2,1,0:T(2,128)S(1)}, u32[]{:S(2)}, u32[]{:S(2)}) async-start(f32[128,2,5]{2,1,0:T(2,128)} %broadcast_multiply_fusion.3), calls=%async_computation | async-start | bytes 262144 | tf_op jit(solution)/shard_map/all_to_all | solution.py:53
  97.2 0.7 copy-start.4
  97.8 27.3 %all-to-all-start.1 = ((f32[128,2,128]{2,1,0:T(2,128)}), f32[128,2,128]{2,1,0:T(2,128)S(1)}, u32[]{:S(2)}, u32[]{:S(2)}) async-start(f32[128,2,128]{2,1,0:T(2,128)} %broadcast_multiply_fusion.2), calls=%async_computation.1 | async-start | bytes 262144 | tf_op jit(solution)/shard_map/all_to_all | solution.py:52
  113.0 18.4 %copy-start.5 = (f32[128,2,5]{2,1,0:T(2,128)S(1)}, f32[128,2,5]{2,1,0:T(2,128)}, u32[]{:S(2)}) copy-start(f32[128,2,5]{2,1,0:T(2,128)} %copy-done.4) | copy-start | bytes 15364
  125.1 36.7 %all-to-all-start.3 = ((f32[128,2,8,128]{3,2,1,0:T(8,128)}), f32[128,2,8,128]{3,2,1,0:T(8,128)S(1)}, u32[]{:S(2)}, u32[]{:S(2)}) async-start(f32[128,2,8,128]{3,2,1,0:T(8,128)} %get-tuple-element.40), calls=%async_computation.3 | async-start | bytes 2097152 | tf_op jit(solution)/shard_map/all_to_all | solution.py:51
  161.8 48.3 %all-to-all-start.2 = ((f32[128,2,8,128]{3,2,1,0:T(8,128)}), f32[128,2,8,128]{3,2,1,0:T(8,128)S(1)}, u32[]{:S(2)}, u32[]{:S(2)}) async-start(f32[128,2,8,128]{3,2,1,0:T(8,128)} %get-tuple-element.39), calls=%async_computation.2 | async-start | bytes 2097152 | tf_op jit(solution)/shard_map/all_to_all | solution.py:50
  210.6 5.6 %copy-start.1 = (f32[128,2,8,128]{3,1,0,2:T(2,128)}, f32[128,2,8,128]{3,1,0,2:T(2,128)S(1)}, u32[]{:S(2)}) copy-start(f32[128,2,8,128]{3,1,0,2:T(2,128)S(1)} %copy.117) | copy-start | bytes 3145732
  214.5 3.3 copy-start.3
  216.2 2.2 copy-start.9
  221.5 8.4 %copy-start.8 = (s32[1024]{0:T(1024)S(1)}, s32[1024]{0:T(1024)}, u32[]{:S(2)}) copy-start(s32[1024]{0:T(1024)} %get-tuple-element.43) | copy-start | bytes 12292
  223.5 4.7 %copy-start.2 = (f32[256,8,128]{2,0,1:T(8,128)S(1)}, f32[256,8,128]{2,0,1:T(8,128)}, u32[]{:S(2)}) copy-start(f32[256,8,128]{2,0,1:T(8,128)} %get-tuple-element.28) | copy-start | bytes 3145732
  240.8 9.3 %copy-start.6 = (f32[256,128]{1,0:T(8,128)S(1)}, f32[256,128]{1,0:T(8,128)}, u32[]{:S(2)}) copy-start(f32[256,128]{1,0:T(8,128)} %get-tuple-element.33) | copy-start | bytes 393220
  258.5 23.0 %copy-start.12 = (s32[256]{0:T(256)S(1)}, s32[256]{0:T(256)}, u32[]{:S(2)}) copy-start(s32[256]{0:T(256)} %get-tuple-element.15) | copy-start | bytes 3076
  281.6 21.5 %copy-start.11 = (s32[256]{0:T(256)S(1)}, s32[256]{0:T(256)}, u32[]{:S(2)}) copy-start(s32[256]{0:T(256)} %get-tuple-element.16) | copy-start | bytes 3076
  303.1 22.7 %copy-start.10 = (s32[256]{0:T(256)S(1)}, s32[256]{0:T(256)}, u32[]{:S(2)}) copy-start(s32[256]{0:T(256)} %get-tuple-element.13) | copy-start | bytes 3076
  350.7 9.1 %copy-start.13 = (s32[112]{0:T(128)S(1)}, s32[112]{0:T(128)}, u32[]{:S(2)}) copy-start(s32[112]{0:T(128)} %get-tuple-element.17) | copy-start | bytes 1348
  352.0 38.2 %all-to-all-start.4 = ((f32[128,2,8,128]{3,1,2,0:T(2,128)}), f32[128,2,8,128]{3,1,2,0:T(2,128)S(1)}, u32[]{:S(2)}, u32[]{:S(2)}) async-start(f32[128,2,8,128]{3,1,2,0:T(2,128)} %copy.143), calls=%async_computation.4 | async-start | bytes 2097152 | tf_op jit(solution)/shard_map/all_to_all | solution.py:92
  359.8 62.7 %all-gather.9.cloned.1.call-start = ((), (), s32[]{:S(2)}) async-start(), calls=%async_computation.7 | async-start | bytes 2293760 | tf_op jit(solution)/shard_map/all_gather | solution.py:97
Sparse Core Ops, SparseCore 0:
  9.5 42.2 all-gather.6
  53.9 38.6 all-gather.4
  391.9 30.4 all-gather.8
where the time goes:
time: 439 us; the launch traced here: 433 us
  waiting for transfers between devices  167 us (38%)
  other arithmetic  101 us (23%)
  starting transfers between devices  65.5 us (15%)
  local copies, waits for them, and re-layouts  63.7 us (15%)
  matrix products  21.7 us (5%)
  between operations  13.7 us (3%)
    scatter-add x4, other arithmetic, local(): jax.ops.segment_sum(traction, target, num_segments=slot_count)  74.7 us
    all_gather x1, waiting for transfers between devices, local(): lax.all_gather(surface_state, 'rep', axis=1, tiled=True)  38.3 us
    all_gather x1, waiting for transfers between devices, local(): lax.all_gather(own_tangent, 'rep', axis=1, tiled=True)  30.6 us
    all_to_all x1, waiting for transfers between devices, local(): lax.all_to_all(summed, 'vol', split_axis=0, concat_axis=0, tiled=True)  30.4 us
    all_to_all x1, waiting for transfers between devices, local(): lax.all_to_all(pack(moving), 'vol', split_axis=0, concat_axis=0, tiled=True)  30 us
    all_to_all x1, starting transfers between devices, local(): lax.all_to_all(send_labels, 'vol', split_axis=0, concat_axis=0, tiled=True)  18.4 us
    all_gather x1, waiting for transfers between devices, local(): moving = fold_one(lax.all_gather(direction, 'rep', axis=1, tiled=True))  17.9 us
    all_to_all x1, starting transfers between devices, local(): lax.all_to_all(pack(projected), 'vol', split_axis=0, concat_axis=0, tiled...  17.9 us
  transfers between devices with their start and end apart: 8, of which 7 were waited for; matrix products, arithmetic and copies ran while one was open for 9% of the time, Pallas kernels for 0%

commit v1 on v0

v1 whole, which is shorter than its diff:
```python
import jax
import jax.numpy as jnp
from jax import lax
from jax.experimental import pallas as pl
from jax.experimental.pallas import tpu as pltpu
from jax.sharding import PartitionSpec as P

SHARPNESS = 1.5
BLOCKS = 112
CH = 8
FACES = 128
REPS = 4
NY = 8
NZC = 16
PARTNERS = 4
ROWS = BLOCKS * CH
HALF = ROWS // 2
F32 = jnp.float32
BF16 = jnp.bfloat16
MESH = pl.DeviceIdType.MESH


def split(x):
    high = x.astype(BF16)
    return high, (x - high.astype(F32)).astype(BF16)


def dot(a, b):
    return jnp.dot(a, b, preferred_element_type=F32)


def body(
    state,
    move,
    stiff_in,
    partners_in,
    owner_in,
    proj,
    mortar_in,
    out,
    gs,
    gd,
    orow,
    lab,
    sti,
    pick,
    pick_t,
    prj,
    mp0,
    mq0,
    ms0,
    mo0,
    mp1,
    mq1,
    ms1,
    mo1,
    labs,
    stis,
    g,
    gt,
    wfs,
    wts,
    mm,
    ml,
    mth,
    mtl,
    p0,
    q0,
    o0,
    p1,
    q1,
    o1,
    own,
    go,
    xs_send,
    xs_recv,
    x_local,
    c_send,
    c_recv,
    c_local,
):
    vol = lax.axis_index("vol")
    rep = lax.axis_index("rep")
    y = vol // NZC
    zc = lax.rem(vol, NZC)
    z = zc // 2
    core = lax.rem(zc, 2)
    right = lax.rem(rep + 1, REPS)
    left = lax.rem(rep + 3, REPS)

    def zc_peer(o):
        return lax.rem(z + o // 2, NY) * 2 + lax.rem(core + lax.rem(o, 2), 2)

    def y_peer(o):
        return lax.rem(y + o, NY)

    barrier = pltpu.get_barrier_semaphore()
    for side in (right, left):
        pl.semaphore_signal(barrier, inc=1, device_id=(vol, side), device_id_type=MESH)

    def greet_z(o, carry):
        peer = y * NZC + zc_peer(o)
        pl.semaphore_signal(barrier, inc=1, device_id=(peer, rep), device_id_type=MESH)
        return carry

    def greet_y(o, carry):
        peer = y_peer(o) * NZC + zc
        pl.semaphore_signal(barrier, inc=1, device_id=(peer, rep), device_id_type=MESH)
        return carry

    lax.fori_loop(1, NZC, greet_z, 0)
    lax.fori_loop(1, NY, greet_y, 0)
    pl.semaphore_wait(barrier, 2 + NZC - 1 + NY - 1)

    first = pl.ds(0, HALF)
    second = pl.ds(HALF, HALF)

    def x_copy(src, dst, n, index, side):
        copy = pltpu.make_async_remote_copy(
            src_ref=src,
            dst_ref=dst,
            send_sem=xs_send.at[n, index],
            recv_sem=xs_recv.at[n, index],
            device_id=(vol, side),
            device_id_type=MESH,
        )
        copy.start()
        return copy

    def x_start(src, dst, n):
        return [
            x_copy(src.at[first], dst.at[rep, first], n, 0, right),
            x_copy(src.at[second], dst.at[rep, second], n, 1, left),
            x_copy(src.at[second], dst.at[rep, second], n, 2, right),
            x_copy(src.at[first], dst.at[rep, first], n, 3, left),
        ]

    def x_relay(dst, n, copies):
        copies[0].wait_recv()
        copies.append(x_copy(dst.at[left, first], dst.at[left, first], n, 4, right))
        copies[1].wait_recv()
        copies.append(x_copy(dst.at[right, second], dst.at[right, second], n, 5, left))

    def x_finish(copies):
        for copy in copies[2:]:
            copy.wait_recv()

    def z_phase(src, dst, sem):
        def one(o, carry):
            peer = zc_peer(o)
            pltpu.make_async_remote_copy(
                src_ref=src(peer),
                dst_ref=dst(zc),
                send_sem=c_send.at[sem],
                recv_sem=c_recv.at[sem],
                device_id=(y * NZC + peer, rep),
                device_id_type=MESH,
            ).start()
            return carry

        lax.fori_loop(1, NZC, one, 0)
        local = pltpu.make_async_copy(src(zc), dst(zc), c_local.at[sem])
        local.start()
        return local

    def y_phase(src, dst, sem):
        def one(o, carry):
            peer = y_peer(o)
            pltpu.make_async_remote_copy(
                src_ref=src(peer),
                dst_ref=dst(y),
                send_sem=c_send.at[sem],
                recv_sem=c_recv.at[sem],
                device_id=(peer * NZC + zc, rep),
                device_id_type=MESH,
            ).start()
            return carry

        lax.fori_loop(1, NY, one, 0)
        local = pltpu.make_async_copy(src(y), dst(y), c_local.at[sem])
        local.start()
        return local

    def drain(local, ref, count, sem):
        whole = pltpu.make_async_remote_copy(
            src_ref=ref.at[pl.ds(0, count)],
            dst_ref=ref.at[pl.ds(0, count)],
            send_sem=c_send.at[sem],
            recv_sem=c_recv.at[sem],
            device_id=(vol, right),
            device_id_type=MESH,
        )
        local.wait()
        whole.wait_recv()
        whole.wait_send()

    copies_s = x_start(state, gs, 0)
    local_s = pltpu.make_async_copy(state, gs.at[rep], x_local.at[0])
    local_s.start()

    lane = lax.broadcasted_iota(jnp.int32, (128, 128), 1)
    row = lax.broadcasted_iota(jnp.int32, (128, 128), 0)
    orow[...] = jnp.full((8, 128), -1.0, F32)
    orow[0:1, 0:BLOCKS] = owner_in[...].astype(F32)
    across = jnp.broadcast_to(orow[0:1, :], (128, 128))
    down = across.T
    rank = jnp.sum(jnp.where((across == down) & (row < lane), 1.0, 0.0), axis=0, keepdims=True)
    dest0 = (lax.rem(row, NY) * NZC + row // NY).astype(F32)
    dest1 = row.astype(F32)
    pick0 = jnp.where((across == dest0) & (rank == 0.0), 1.0, 0.0)
    pick1 = jnp.where((across == dest1) & (rank == 1.0), 1.0, 0.0)
    pick[0:128, 0:128] = pick0.astype(BF16)
    pick[0:128, 128:256] = pick0.astype(BF16)
    pick[128:256, 0:128] = pick1.astype(BF16)
    pick[128:256, 128:256] = pick1.astype(BF16)
    pick_t[:, 0:128] = pick0.T.astype(BF16)
    pick_t[:, 128:256] = pick1.T.astype(BF16)

    lab[...] = jnp.zeros((128, 128), F32)
    lab[0:BLOCKS, 0:PARTNERS] = (partners_in[...] + 1).astype(F32)
    ids = lax.broadcasted_iota(jnp.int32, (BLOCKS, 1), 0) + (vol * BLOCKS + 1)
    lab[0:BLOCKS, PARTNERS : PARTNERS + 1] = ids.astype(F32)
    sti[...] = jnp.zeros((128, 128), F32)
    sti[0:BLOCKS, :] = stiff_in[...]

    def packed(x):
        high, low = split(x)
        return dot(pick[...], jnp.concatenate([high, low], axis=0))

    for kind, source in ((0, sti), (1, lab)):
        rows = packed(source[...])
        for i in range(NZC):
            mp0[i, kind] = rows[i * NY : (i + 1) * NY]
        for i in range(NY):
            mp1[i, kind] = rows[128 + i * NZC : 128 + (i + 1) * NZC]
    meta0 = z_phase(lambda i: mp0.at[i], lambda i: mq0.at[i], 0)
    meta1 = y_phase(lambda i: mp1.at[i], lambda i: mq1.at[i], 1)

    for k in range(PARTNERS):
        cols = slice(k * FACES, (k + 1) * FACES)
        high, low = split(mortar_in[k])
        mm[0:FACES, cols] = high
        mm[FACES : 2 * FACES, cols] = high
        ml[:, cols] = low
        high, low = split(mortar_in[k].T)
        mth[k, 0:FACES, :] = high
        mth[k, FACES : 2 * FACES, :] = high
        mtl[k] = low
    prj[...] = jnp.zeros((CH, 128, FACES), F32)

    x_relay(gs, 0, copies_s)
    copies_d = x_start(move, gd, 1)
    local_d = pltpu.make_async_copy(move, gd.at[rep], x_local.at[1])
    local_d.start()

    drain(meta0, mq0, NZC - 1, 0)
    drain(meta1, mq1, NY - 1, 1)
    flat0 = mq0.reshape(NZC * 2 * NY, FACES)
    flat1 = mq1.reshape(NY * 2 * NZC, FACES)
    for kind in range(2):
        for i in range(NY):
            ms0[i, kind] = flat0[pl.ds(kind * NY + i, NZC, stride=2 * NY), :]
        for i in range(NZC):
            ms1[i, kind] = flat1[pl.ds(kind * NZC + i, NY, stride=2 * NZC), :]
    meta0 = y_phase(lambda i: ms0.at[i], lambda i: mo0.at[i], 2)
    meta1 = z_phase(lambda i: ms1.at[i], lambda i: mo1.at[i], 3)

    def project(gathered, transposed):
        for start in (0, 56):
            for base in (0, 4):
                total = [jnp.zeros((56, FACES), F32) for _ in range(4)]
                for j in range(REPS * CH):
                    x = gathered[j // CH, pl.ds(start * CH + j % CH, 56, stride=CH), :]
                    for i in range(4):
                        if transposed:
                            factor = proj[j, rep * CH + base + i]
                        else:
                            factor = proj[rep * CH + base + i, j]
                        total[i] = total[i] + factor * x
                yield start, base, total

    def pack_field(gathered, n):
        for start, base, total in project(gathered, False):
            for i in range(4):
                prj[base + i, start : start + 56, :] = total[i]
        dst0 = p0.at[n].reshape(128 * CH, FACES)
        dst1 = p1.at[n].reshape(128 * CH, FACES)
        for i in range(CH):
            rows = packed(prj[i])
            dst0[pl.ds(i, 128, stride=CH), :] = rows[0:128]
            dst1[pl.ds(i, 128, stride=CH), :] = rows[128:256]

    def phase_one(n):
        sem = 4 + 4 * n
        a = z_phase(lambda i: p0.at[n, i], lambda i: q0.at[n, i], sem)
        b = y_phase(lambda i: p1.at[n, i], lambda i: q1.at[n, i], sem + 1)
        return a, b

    def phase_two(n, started):
        sem = 4 + 4 * n
        drain(started[0], q0.at[n], NZC - 1, sem)
        a = y_phase(lambda i: q0.at[n, :, i], lambda i: o0.at[n, i], sem + 2)
        drain(started[1], q1.at[n], NY - 1, sem + 1)
        b = z_phase(lambda i: q1.at[n, :, i], lambda i: o1.at[n, i], sem + 3)
        return a, b

    def phase_end(n, started):
        sem = 4 + 4 * n
        drain(started[0], o0.at[n], NY - 1, sem + 2)
        drain(started[1], o1.at[n], NZC - 1, sem + 3)

    x_finish(copies_s)
    local_s.wait()
    pack_field(gs, 0)
    run_s = phase_one(0)
    x_relay(gd, 1, copies_d)

    drain(meta0, mo0, NY - 1, 2)
    drain(meta1, mo1, NZC - 1, 3)
    for i in range(NY):
        stis[i * NZC : (i + 1) * NZC] = mo0[i, 0]
        labs[i * NZC : (i + 1) * NZC] = mo0[i, 1]
    for i in range(NZC):
        stis[128 + i * NY : 128 + (i + 1) * NY] = mo1[i, 0]
        labs[128 + i * NY : 128 + (i + 1) * NY] = mo1[i, 1]
    labels = labs[...]
    turned = labels.T
    ones = jnp.ones((256, FACES), BF16)
    for k in range(PARTNERS):
        hit = labels[:, k : k + 1] == turned[PARTNERS : PARTNERS + 1, :]
        g[k] = jnp.where(hit, 1.0, 0.0).astype(BF16)
        hit = labels[:, PARTNERS : PARTNERS + 1] == turned[k : k + 1, :]
        gt[k] = jnp.where(hit, 1.0, 0.0).astype(BF16)
        wfs[k] = dot(g[k], ones) * stis[...] * SHARPNESS

    run_s = phase_two(0, run_s)
    x_finish(copies_d)
    local_d.wait()
    pack_field(gd, 1)
    run_d = phase_one(1)
    phase_end(0, run_s)

    def received(n, i):
        a = o0.at[n].reshape(128 * CH, FACES)[pl.ds(i, 128, stride=CH), :]
        b = o1.at[n].reshape(128 * CH, FACES)[pl.ds(i, 128, stride=CH), :]
        return jnp.concatenate([a, b], axis=0)

    def mapped(x):
        high, low = split(x)
        total = dot(jnp.concatenate([high, low], axis=1), mm[...]) + dot(high, ml[...])
        result = []
        for k in range(PARTNERS):
            high, low = split(total[:, k * FACES : (k + 1) * FACES])
            both = dot(g[k], jnp.concatenate([high, low], axis=1))
            result.append(both[:, 0:FACES] + both[:, FACES:])
        return result

    def weigh(i, carry):
        x = received(0, i)
        for k, partner in enumerate(mapped(x)):
            squashed = 1.0 / (1.0 + jnp.exp(-SHARPNESS * (x - partner)))
            wts[i, k] = wfs[k] * squashed * (1.0 - squashed)
        return carry

    lax.fori_loop(0, CH, weigh, 0)
    run_d = phase_two(1, run_d)
    phase_end(1, run_d)

    back1 = p1.at[2].reshape(128 * CH, FACES)
    back0 = p0.at[2].reshape(128 * CH, FACES)

    def pull(i, carry):
        x = received(1, i)
        total = jnp.zeros((256, FACES), F32)
        for k, partner in enumerate(mapped(x)):
            traction = wts[i, k] * (x - partner)
            total = total + traction
            high, low = split(traction)
            both = dot(gt[k], jnp.concatenate([high, low], axis=1))
            high, low = split(both[:, 0:FACES] + both[:, FACES:])
            total = total - dot(jnp.concatenate([high, low], axis=1), mth[k]) - dot(high, mtl[k])
        back1[pl.ds(i, 128, stride=CH), :] = total[0:128]
        back0[pl.ds(i, 128, stride=CH), :] = total[128:256]
        return carry

    lax.fori_loop(0, CH, pull, 0)
    run_r = phase_one(2)
    run_r = phase_two(2, run_r)
    phase_end(2, run_r)

    home = own
    for i in range(CH):
        a = o1.at[2].reshape(128 * CH, FACES)[pl.ds(i, 128, stride=CH), :]
        b = o0.at[2].reshape(128 * CH, FACES)[pl.ds(i, 128, stride=CH), :]
        high, low = split(jnp.concatenate([a, b], axis=0))
        both = dot(pick_t[...], jnp.concatenate([high, low], axis=1))
        both = both[:, 0:FACES] + both[:, FACES:]
        home[pl.ds(i, BLOCKS, stride=CH), :] = both[0:BLOCKS]
    copies_o = x_start(own, go, 2)
    local_o = pltpu.make_async_copy(own, go.at[rep], x_local.at[2])
    local_o.start()
    x_relay(go, 2, copies_o)
    x_finish(copies_o)
    local_o.wait()
    for start, base, total in project(go, True):
        for i in range(4):
            out[pl.ds(start * CH + base + i, 56, stride=CH), :] = total[i]
    for copy in copies_s + copies_d + copies_o:
        copy.wait_send()


def local(surface_state, direction, stiffness, partners, contact_owner, projection, mortar):
    vmem = pl.BlockSpec(memory_space=pltpu.VMEM)
    anywhere = pl.BlockSpec(memory_space=pl.ANY)
    result = pl.pallas_call(
        body,
        out_shape=jax.ShapeDtypeStruct((ROWS, FACES), F32),
        in_specs=[
            anywhere,
            anywhere,
            vmem,
            vmem,
            vmem,
            pl.BlockSpec(memory_space=pltpu.SMEM),
            vmem,
        ],
        out_specs=vmem,
        scratch_shapes=[
            pltpu.VMEM((REPS, ROWS, FACES), F32),
            pltpu.VMEM((REPS, ROWS, FACES), F32),
            pltpu.VMEM((8, 128), F32),
            pltpu.VMEM((128, 128), F32),
            pltpu.VMEM((128, FACES), F32),
            pltpu.VMEM((256, 256), BF16),
            pltpu.VMEM((128, 256), BF16),
            pltpu.VMEM((CH, 128, FACES), F32),
            pltpu.VMEM((NZC, 2, NY, FACES), F32),
            pltpu.VMEM((NZC, 2, NY, FACES), F32),
            pltpu.VMEM((NY, 2, NZC, FACES), F32),
            pltpu.VMEM((NY, 2, NZC, FACES), F32),
            pltpu.VMEM((NY, 2, NZC, FACES), F32),
            pltpu.VMEM((NY, 2, NZC, FACES), F32),
            pltpu.VMEM((NZC, 2, NY, FACES), F32),
            pltpu.VMEM((NZC, 2, NY, FACES), F32),
            pltpu.VMEM((256, 128), F32),
            pltpu.VMEM((256, FACES), F32),
            pltpu.VMEM((PARTNERS, 256, 256), BF16),
            pltpu.VMEM((PARTNERS, 256, 256), BF16),
            pltpu.VMEM((PARTNERS, 256, FACES), F32),
            pltpu.VMEM((CH, PARTNERS, 256, FACES), F32),
            pltpu.VMEM((256, PARTNERS * FACES), BF16),
            pltpu.VMEM((128, PARTNERS * FACES), BF16),
            pltpu.VMEM((PARTNERS, 256, FACES), BF16),
            pltpu.VMEM((PARTNERS, 128, FACES), BF16),
            pltpu.VMEM((3, NZC, NY, CH, FACES), F32),
            pltpu.VMEM((3, NZC, NY, CH, FACES), F32),
            pltpu.VMEM((3, NY, NZC, CH, FACES), F32),
            pltpu.VMEM((3, NY, NZC, CH, FACES), F32),
            pltpu.VMEM((3, NY, NZC, CH, FACES), F32),
            pltpu.VMEM((3, NZC, NY, CH, FACES), F32),
            pltpu.VMEM((ROWS, FACES), F32),
            pltpu.VMEM((REPS, ROWS, FACES), F32),
            pltpu.SemaphoreType.DMA((3, 6)),
            pltpu.SemaphoreType.DMA((3, 6)),
            pltpu.SemaphoreType.DMA((3,)),
            pltpu.SemaphoreType.DMA((16,)),
            pltpu.SemaphoreType.DMA((16,)),
            pltpu.SemaphoreType.DMA((16,)),
        ],
        compiler_params=pltpu.CompilerParams(
            collective_id=0, has_side_effects=True, vmem_limit_bytes=60 * 1024 * 1024
        ),
        name="contact",
    )(
        surface_state.reshape(ROWS, FACES),
        direction.reshape(ROWS, FACES),
        stiffness,
        partners,
        contact_owner.reshape(1, BLOCKS),
        projection,
        mortar,
    )
    return result.reshape(BLOCKS, CH, FACES)


def solution(mesh):
    placed = (
        P("vol", "rep", None),
        P("vol", "rep", None),
        P("vol", None),
        P("vol", None),
        P("vol"),
        P(),
        P(),
    )
    return jax.shard_map(
        local, mesh=mesh, in_specs=placed, out_specs=P("vol", "rep", None), check_vma=False
    )
```

time: 439 us -> 151 us (0.34); the launches traced: 433 us -> 151 us
  waiting for transfers between devices: 167 us -> 0 us
  Pallas kernels: 0 us -> 148 us
  other arithmetic: 101 us -> 0 us
  starting transfers between devices: 65.5 us -> 0 us
  local copies, waits for them, and re-layouts: 63.7 us -> 3.23 us
  matrix products: 21.7 us -> 0 us
  between operations: 13.7 us -> 0.01 us
    pallas_call x0 -> x1, Pallas kernels: none -> 148 us  [local(): pl.pallas_call(body, out_shape=jax.ShapeDtypeStruct((ROWS, FACES), F32),...]
    all_gather x3 -> x0, waiting for transfers between devices: 86.9 us -> none  [the longest x1 38.3 us: local(): lax.all_gather(surface_state, 'rep', axis=1, tiled=True)]
    all_to_all x5 -> x0, waiting for transfers between devices: 78.8 us -> none  [the longest x1 30.4 us: local(): lax.all_to_all(summed, 'vol', split_axis=0, concat_axis=0, tiled=True)]
    scatter-add x4 -> x0, other arithmetic: 74.7 us -> none  [local(): jax.ops.segment_sum(traction, target, num_segments=slot_count)]
    all_to_all x5 -> x0, starting transfers between devices: 65.5 us -> none  [the longest x1 18.4 us: local(): lax.all_to_all(send_labels, 'vol', split_axis=0, concat_axis=0, tiled=True)]
    gather x14 -> x0, local copies, waits for them, and re-layouts: 29.3 us -> none  [the longest x4 11.4 us: local(): contact_gap = got_state - mapped_state[column][target]]
    dot_general x6 -> x0, matrix products: 21.7 us -> none  [the longest x1 6.09 us: local(): jnp.einsum('krcg,kfg->rcf', jnp.stack(returns), mortar, precision=highest)]
    squeeze x10 -> x0, local copies, waits for them, and re-layouts: 17.3 us -> none  [the longest x5 10.8 us: local(): contact_gap = got_state - mapped_state[column][target]]
  transfers between devices with their start and end apart: 8 -> 0, of which waited for: 7 -> 0; matrix products, arithmetic and copies ran while one was open for 9% -> 0% of each run, Pallas kernels for 0% -> 0%
where the time goes in v1:
time: 151 us
  Pallas kernels  148 us (98%)
  local copies, waits for them, and re-layouts  3.23 us (2%)
    pallas_call x1, Pallas kernels, local(): pl.pallas_call(body, out_shape=jax.ShapeDtypeStruct((ROWS, FACES), F32),...  148 us
    unnamed x4, local copies, waits for them, and re-layouts  3.23 us

profile of v1, /device:TPU:1, one launch (start us, length us, event | category | flops | bytes accessed | tf_op | source)
XLA Modules:
  0.0 151.2 jit_solution(3596719739941665642)
XLA Ops:
  0.0 0.0 copy-start
  0.0 0.7 copy-done
  0.7 0.7 copy.8.partners_in
  1.4 148.0 %contact.1 = f32[896,128]{1,0:T(8,128)} custom-call(f32[896,128]{1,0:T(8,128)} %bitcast.5, f32[896,128]{1,0:T(8,128)} %bitcast.6, f32[112,128]{1,0:T(8,128)} %stiff_in.1, s32[112,4]{1,0:T(8,128)} %copy.8.partners_in, s32[1,112]{1,0:T(1,128)} %bitcast.7, f32[32,32]{1,0:T(8,128)} %proj.1, f32[4,128,128]{2,1,0:T(8,128)} %mortar_in.1), custom_call_target="tpu_custom_call" | custom-call | tf_op jit(solution)/shard_map/contact/pallas_call | solution.py:415
  149.4 1.8 %copy.10 = f32[112,8,128]{2,1,0:T(8,128)} copy(f32[112,8,128]{2,1,0:T(8,128)} %bitcast.4) | data formatting | bytes 917504
Async XLA Ops:
  0.0 0.7 copy-start

commit v2 on v1

v2 whole, which is shorter than its diff:
```python
import jax
import jax.numpy as jnp
from jax import lax
from jax.experimental import pallas as pl
from jax.experimental.pallas import tpu as pltpu
from jax.sharding import PartitionSpec as P

SHARPNESS = 1.5
BLOCKS = 112
CH = 8
FACES = 128
REPS = 4
NY = 8
NZ = 8
PARTNERS = 4
ROWS = BLOCKS * CH
SLOTS = 128
F32 = jnp.float32
BF16 = jnp.bfloat16
MESH = pl.DeviceIdType.MESH


def split(x):
    high = x.astype(BF16)
    return high, (x - high.astype(F32)).astype(BF16)


def dot(a, b):
    return jnp.dot(a, b, preferred_element_type=F32)


def body(
    state,
    move,
    stiff_in,
    partners_in,
    owner_in,
    proj,
    mortar_in,
    out,
    gs,
    go,
    gd,
    gr,
    gm,
    raw,
    orow,
    lab_t,
    lab,
    sti,
    pick,
    pick_t,
    prj,
    prd,
    mp,
    mq,
    ms,
    labs,
    stis,
    g,
    gta,
    wfs,
    wts,
    uhl,
    tan,
    mm,
    ml,
    mth,
    mtl,
    p,
    q,
    o,
    x_send,
    x_recv,
    x_local,
    c_send,
    c_recv,
    c_local,
):
    vol = lax.axis_index("vol")
    rep = lax.axis_index("rep")
    y = vol // 16
    z = lax.rem(vol // 2, NZ)
    core = lax.rem(vol, 2)
    right = lax.rem(rep + 1, REPS)
    left = lax.rem(rep + 3, REPS)

    def along_z(peer, cross):
        return y * 16 + peer * 2 + (1 - core if cross else core)

    def along_y(peer):
        return peer * 16 + z * 2 + core

    local_s = pltpu.make_async_copy(state, gs.at[rep], x_local.at[0])
    local_s.start()
    local_d = pltpu.make_async_copy(move, raw.at[pl.ds(0, ROWS)], x_local.at[1])
    local_d.start()
    barrier = pltpu.get_barrier_semaphore()
    for side in (right, left):
        pl.semaphore_signal(barrier, inc=1, device_id=(vol, side), device_id_type=MESH)

    def greet(o, carry):
        for peer in (
            along_z(lax.rem(z + o, NZ), False),
            along_z(lax.rem(z + o, NZ), True),
            along_y(lax.rem(y + o, NY)),
        ):
            pl.semaphore_signal(barrier, inc=1, device_id=(peer, rep), device_id_type=MESH)
        return carry

    pl.semaphore_signal(barrier, inc=1, device_id=(along_z(z, True), rep), device_id_type=MESH)
    lax.fori_loop(1, 8, greet, 0)

    lane = lax.broadcasted_iota(jnp.int32, (128, 128), 1)
    row = lax.broadcasted_iota(jnp.int32, (128, 128), 0)
    orow[...] = jnp.full((8, 128), -1.0, F32)
    orow[0:1, 0:BLOCKS] = owner_in[...].astype(F32)
    across = jnp.broadcast_to(orow[0:1, :], (128, 128))
    down = across.T
    rank = jnp.sum(jnp.where((across == down) & (row < lane), 1.0, 0.0), axis=0, keepdims=True)
    major = lax.rem(row // 8, 8)
    minor = lax.rem(row, 8)
    dest = jnp.where(
        row < 64, minor * 16 + major * 2 + core, major * 16 + minor * 2 + (1 - core)
    ).astype(F32)
    for h in range(2):
        chosen = jnp.where((across == dest) & (rank == float(h)), 1.0, 0.0)
        pick[h * 128 : (h + 1) * 128, 0:128] = chosen.astype(BF16)
        pick[h * 128 : (h + 1) * 128, 128:256] = chosen.astype(BF16)
        pick_t[:, h * 128 : (h + 1) * 128] = chosen.T.astype(BF16)

    def x_copy(src, dst, n, index, side):
        copy = pltpu.make_async_remote_copy(
            src_ref=src,
            dst_ref=dst,
            send_sem=x_send.at[n, index],
            recv_sem=x_recv.at[n, index],
            device_id=(vol, side),
            device_id_type=MESH,
        )
        copy.start()
        return copy

    def x_start(own, view, n):
        return [
            x_copy(own(0), view(rep, 0), n, 0, right),
            x_copy(own(1), view(rep, 1), n, 1, left),
            x_copy(own(1), view(rep, 1), n, 2, right),
            x_copy(own(0), view(rep, 0), n, 3, left),
        ]

    def x_relay(view, n, copies):
        copies[0].wait_recv()
        copies.append(x_copy(view(left, 0), view(left, 0), n, 4, right))
        copies[1].wait_recv()
        copies.append(x_copy(view(right, 1), view(right, 1), n, 5, left))

    def x_finish(copies):
        for copy in copies[2:]:
            copy.wait_recv()

    def phase(dim, cross, src, dst, sem):
        mine = z if dim == "z" else y

        def one(i, carry):
            peer = lax.rem(mine + i, 8)
            device = along_z(peer, cross) if dim == "z" else along_y(peer)
            pltpu.make_async_remote_copy(
                src_ref=src(peer),
                dst_ref=dst(mine),
                send_sem=c_send.at[sem],
                recv_sem=c_recv.at[sem],
                device_id=(device, rep),
                device_id_type=MESH,
            ).start()
            return carry

        lax.fori_loop(0 if cross else 1, 8, one, 0)
        if cross:
            return None
        own = pltpu.make_async_copy(src(mine), dst(mine), c_local.at[sem])
        own.start()
        return own

    def drain(own, ref, sem):
        count = 8 if own is None else 7
        whole = pltpu.make_async_remote_copy(
            src_ref=ref.at[pl.ds(0, count)],
            dst_ref=ref.at[pl.ds(0, count)],
            send_sem=c_send.at[sem],
            recv_sem=c_recv.at[sem],
            device_id=(vol, right),
            device_id_type=MESH,
        )
        if own is not None:
            own.wait()
        whole.wait_recv()
        whole.wait_send()

    def there_one(n):
        a = phase("z", False, lambda i: p.at[n, 0, i], lambda i: q.at[n, 0, i], 4 * n)
        b = phase("y", False, lambda i: p.at[n, 1, i], lambda i: q.at[n, 1, i], 4 * n + 1)
        return a, b

    def there_two(n, run, land):
        drain(run[0], q.at[n, 0], 4 * n)
        a = phase("y", False, lambda i: q.at[n, 0, :, i], lambda i: land(0).at[i], 4 * n + 2)
        drain(run[1], q.at[n, 1], 4 * n + 1)
        b = phase("z", True, lambda i: q.at[n, 1, :, i], lambda i: land(1).at[i], 4 * n + 3)
        return a, b

    def there_end(n, run, land):
        drain(run[0], land(0), 4 * n + 2)
        drain(run[1], land(1), 4 * n + 3)

    def back_one(n):
        a = phase("y", False, lambda i: p.at[n, 0, i], lambda i: q.at[n, 0, i], 4 * n)
        b = phase("z", True, lambda i: p.at[n, 1, i], lambda i: q.at[n, 1, i], 4 * n + 1)
        return a, b

    def back_two(n, run):
        drain(run[0], q.at[n, 0], 4 * n)
        a = phase("z", False, lambda i: q.at[n, 0, :, i], lambda i: o.at[n, 0, i], 4 * n + 2)
        drain(run[1], q.at[n, 1], 4 * n + 1)
        b = phase("y", False, lambda i: q.at[n, 1, :, i], lambda i: o.at[n, 1, i], 4 * n + 3)
        return a, b

    def back_end(n, run):
        drain(run[0], o.at[n, 0], 4 * n + 2)
        drain(run[1], o.at[n, 1], 4 * n + 3)

    def put(n, i, rows):
        for part in range(2):
            dst = p.at[n, part].reshape(64 * CH, FACES)
            dst[pl.ds(i, 64, stride=CH), :] = rows[part * 64 : (part + 1) * 64]

    def chosen_rows(rows, x):
        high, low = split(x)
        return dot(rows, jnp.concatenate([high, low], axis=0))

    def gs_view(origin, part):
        return gs.at[origin, pl.ds(part * (ROWS // 2), ROWS // 2)]

    def go_view(origin, part):
        return go.at[origin, pl.ds(part * (ROWS // 2), ROWS // 2)]

    def gr_view(origin, part):
        return gr.at[origin, pl.ds(part * 64 * CH, 64 * CH)]

    def gm_view(origin, part):
        return gm.at[origin, part]

    def gd_view(h):
        return lambda origin, part: gd.at[h, part, origin]

    pl.semaphore_wait(barrier, 24)
    x_state = x_start(
        lambda part: state.at[pl.ds(part * (ROWS // 2), ROWS // 2)], gs_view, 0
    )

    lab_t[...] = jnp.zeros((128, 128), F32)
    lab_t[0:PARTNERS, 0:BLOCKS] = (partners_in[...] + 1).astype(F32)
    count = lax.broadcasted_iota(jnp.int32, (1, 128), 1)
    lab_t[PARTNERS : PARTNERS + 1, :] = jnp.where(
        count < BLOCKS, count + (vol * BLOCKS + 1), 0
    ).astype(F32)
    lab[...] = lab_t[...].T
    sti[...] = jnp.zeros((128, FACES), F32)
    sti[0:BLOCKS, :] = stiff_in[...]
    table = jnp.where(lax.rem(rep, 2) == 0, sti[...], lab[...])
    rows = chosen_rows(pick[pl.ds((rep // 2) * 128, 128), :], table)
    for part in range(2):
        for i in range(8):
            mp[part, i] = rows[part * 64 + i * 8 : part * 64 + (i + 1) * 8]
    meta = (
        phase("z", False, lambda i: mp.at[0, i], lambda i: mq.at[0, i], 24),
        phase("y", False, lambda i: mp.at[1, i], lambda i: mq.at[1, i], 25),
    )

    raw[ROWS:, :] = jnp.zeros((128 * CH - ROWS, FACES), F32)
    local_d.wait()
    runs = []
    for h in range(2):
        for i in range(CH):
            x = raw[pl.ds(i, 128, stride=CH), :]
            put(h, i, chosen_rows(pick[h * 128 : (h + 1) * 128, :], x))
        runs.append(there_one(h))

    drain(meta[0], mq.at[0], 24)
    drain(meta[1], mq.at[1], 25)
    for part in range(2):
        flat = mq.at[part].reshape(64, FACES)
        for i in range(8):
            ms[part, i] = flat[pl.ds(i, 8, stride=8), :]
    meta = (
        phase("y", False, lambda i: ms.at[0, i], lambda i: gm.at[rep, 0, i], 26),
        phase("z", True, lambda i: ms.at[1, i], lambda i: gm.at[rep, 1, i], 27),
    )
    x_relay(gs_view, 0, x_state)

    for k in range(PARTNERS):
        cols = slice(k * FACES, (k + 1) * FACES)
        high, low = split(mortar_in[k])
        mm[0:FACES, cols] = high
        mm[FACES : 2 * FACES, cols] = high
        ml[:, cols] = low
        high, low = split(mortar_in[k].T)
        mth[k, 0:FACES, :] = high
        mth[k, FACES : 2 * FACES, :] = high
        mtl[k] = low
    prj[...] = jnp.zeros((CH, 128, FACES), F32)

    def land_d(h):
        return lambda part: gd.at[h, part, rep]

    runs[0] = there_two(0, runs[0], land_d(0))
    drain(meta[0], gm.at[rep, 0], 26)
    drain(meta[1], gm.at[rep, 1], 27)
    x_meta = x_start(lambda part: gm.at[rep, part], gm_view, 1)
    runs[1] = there_two(1, runs[1], land_d(1))
    there_end(0, runs[0], land_d(0))
    x_d0 = x_start(lambda part: gd.at[0, part, rep], gd_view(0), 2)

    def project(load, count, transposed, base):
        total = [jnp.zeros((count, FACES), F32) for _ in range(4)]
        for j in range(REPS * CH):
            x = load(j)
            for i in range(4):
                if transposed:
                    factor = proj[j, rep * CH + base + i]
                else:
                    factor = proj[rep * CH + base + i, j]
                total[i] = total[i] + factor * x
        return total

    def rows_of(ref, start):
        return lambda j: ref[j // CH, pl.ds(start * CH + j % CH, 56, stride=CH), :]

    x_finish(x_state)
    local_s.wait()
    for start in (0, 56):
        for base in (0, 4):
            total = project(rows_of(gs, start), 56, False, base)
            for i in range(4):
                prj[base + i, start : start + 56, :] = total[i]
    for h in range(2):
        for i in range(CH):
            put(2 + h, i, chosen_rows(pick[h * 128 : (h + 1) * 128, :], prj[i]))
        runs.append(there_one(2 + h))

    x_relay(gm_view, 1, x_meta)
    x_finish(x_meta)
    for h in range(2):
        stis[h * 128 : (h + 1) * 128] = gm.at[2 * h].reshape(128, FACES)[...]
        labs[h * 128 : (h + 1) * 128] = gm.at[2 * h + 1].reshape(128, FACES)[...]
    labels = labs[...]
    turned = labels.T
    ones = jnp.ones((256, FACES), BF16)
    for k in range(PARTNERS):
        hit = labels[:, k : k + 1] == turned[PARTNERS : PARTNERS + 1, :]
        g[k] = jnp.where(hit, 1.0, 0.0).astype(BF16)
        hit = labels[:, PARTNERS : PARTNERS + 1] == turned[k : k + 1, :]
        gta[:, k * 256 : (k + 1) * 256] = jnp.where(hit, 1.0, 0.0).astype(BF16)
        wfs[k] = dot(g[k], ones) * stis[...] * SHARPNESS

    x_relay(gd_view(0), 2, x_d0)
    there_end(1, runs[1], land_d(1))
    x_d1 = x_start(lambda part: gd.at[1, part, rep], gd_view(1), 3)

    def land(n):
        return lambda part: o.at[n, part]

    runs[2] = there_two(2, runs[2], land(2))

    def project_slots(h):
        for part in range(2):

            def load(j):
                flat = gd.at[h, part, j // CH].reshape(64 * CH, FACES)
                return flat[pl.ds(j % CH, 64, stride=CH), :]

            for base in (0, 4):
                total = project(load, 64, False, base)
                start = h * 128 + part * 64
                for i in range(4):
                    prd[base + i, start : start + 64, :] = total[i]

    x_finish(x_d0)
    project_slots(0)
    runs[3] = there_two(3, runs[3], land(3))
    x_relay(gd_view(1), 3, x_d1)

    def mapped(x):
        high, low = split(x)
        total = dot(jnp.concatenate([high, low], axis=1), mm[...]) + dot(high, ml[...])
        result = []
        for k in range(PARTNERS):
            high, low = split(total[:, k * FACES : (k + 1) * FACES])
            both = dot(g[k], jnp.concatenate([high, low], axis=1))
            result.append(both[:, 0:FACES] + both[:, FACES:])
        return result

    def weigh(i, carry):
        x = jnp.concatenate(
            [
                o.at[2 + h, part].reshape(64 * CH, FACES)[pl.ds(i, 64, stride=CH), :]
                for h in range(2)
                for part in range(2)
            ],
            axis=0,
        )
        for k, partner in enumerate(mapped(x)):
            squashed = 1.0 / (1.0 + jnp.exp(-SHARPNESS * (x - partner)))
            wts[i, k] = wfs[k] * squashed * (1.0 - squashed)
        return carry

    there_end(2, runs[2], land(2))
    there_end(3, runs[3], land(3))
    lax.fori_loop(0, CH, weigh, 0)
    x_finish(x_d1)
    project_slots(1)

    def pull(i, carry):
        x = prd[i]
        total = jnp.zeros((256, FACES), F32)
        for k, partner in enumerate(mapped(x)):
            traction = wts[i, k] * (x - partner)
            total = total + traction
            high, low = split(traction)
            pulled = dot(jnp.concatenate([high, low], axis=1), mth[k]) + dot(high, mtl[k])
            high, low = split(pulled)
            uhl[i, k * 256 : (k + 1) * 256, :] = jnp.concatenate([high, low], axis=1)
        tan[i] = total
        return carry

    def summed(i, h):
        both = dot(gta[h * 128 : (h + 1) * 128, :], uhl[i])
        return tan[i, h * 128 : (h + 1) * 128, :] - both[:, 0:FACES] - both[:, FACES:]

    lax.fori_loop(0, CH, pull, 0)
    mine = gr.at[rep]
    for i in range(CH):
        mine[pl.ds(i, 128, stride=CH), :] = summed(i, 1)
    x_back = x_start(lambda part: gr_view(rep, part), gr_view, 4)
    for i in range(CH):
        put(4, i, summed(i, 0))
    run_first = back_one(4)
    x_relay(gr_view, 4, x_back)
    run_first = back_two(4, run_first)
    x_finish(x_back)
    for part in range(2):

        def load(j):
            return gr[j // CH, pl.ds(part * 64 * CH + j % CH, 64, stride=CH), :]

        dst = p.at[5, part].reshape(64 * CH, FACES)
        for base in (0, 4):
            total = project(load, 64, True, base)
            for i in range(4):
                dst[pl.ds(base + i, 64, stride=CH), :] = total[i]
    run_second = back_one(5)
    back_end(4, run_first)

    def home(n, i):
        x = jnp.concatenate(
            [
                o.at[n, part].reshape(64 * CH, FACES)[pl.ds(i, 64, stride=CH), :]
                for part in range(2)
            ],
            axis=0,
        )
        high, low = split(x)
        h = n - 4
        both = dot(pick_t[:, h * 128 : (h + 1) * 128], jnp.concatenate([high, low], axis=1))
        return (both[:, 0:FACES] + both[:, FACES:])[0:BLOCKS]

    mine = go.at[rep]
    for i in range(CH):
        mine[pl.ds(i, BLOCKS, stride=CH), :] = home(4, i)
    x_home = x_start(lambda part: go_view(rep, part), go_view, 5)
    run_second = back_two(5, run_second)
    x_relay(go_view, 5, x_home)
    back_end(5, run_second)
    for i in range(CH):
        prj[i, 0:BLOCKS, :] = home(5, i)
    x_finish(x_home)
    for start in (0, 56):
        for base in (0, 4):
            total = project(rows_of(go, start), 56, True, base)
            for i in range(4):
                out[pl.ds(start * CH + base + i, 56, stride=CH), :] = (
                    total[i] + prj[base + i, start : start + 56, :]
                )
    for copy in x_state + x_meta + x_d0 + x_d1 + x_back + x_home:
        copy.wait_send()


def local(surface_state, direction, stiffness, partners, contact_owner, projection, mortar):
    vmem = pl.BlockSpec(memory_space=pltpu.VMEM)
    anywhere = pl.BlockSpec(memory_space=pl.ANY)
    result = pl.pallas_call(
        body,
        out_shape=jax.ShapeDtypeStruct((ROWS, FACES), F32),
        in_specs=[
            anywhere,
            anywhere,
            vmem,
            vmem,
            vmem,
            pl.BlockSpec(memory_space=pltpu.SMEM),
            vmem,
        ],
        out_specs=vmem,
        scratch_shapes=[
            pltpu.VMEM((REPS, ROWS, FACES), F32),
            pltpu.VMEM((REPS, ROWS, FACES), F32),
            pltpu.VMEM((2, 2, REPS, 8, 8, CH, FACES), F32),
            pltpu.VMEM((REPS, SLOTS * CH, FACES), F32),
            pltpu.VMEM((REPS, 2, 8, 8, FACES), F32),
            pltpu.VMEM((128 * CH, FACES), F32),
            pltpu.VMEM((8, 128), F32),
            pltpu.VMEM((128, 128), F32),
            pltpu.VMEM((128, 128), F32),
            pltpu.VMEM((128, FACES), F32),
            pltpu.VMEM((256, 256), BF16),
            pltpu.VMEM((128, 256), BF16),
            pltpu.VMEM((CH, 128, FACES), F32),
            pltpu.VMEM((CH, 256, FACES), F32),
            pltpu.VMEM((2, 8, 8, FACES), F32),
            pltpu.VMEM((2, 8, 8, FACES), F32),
            pltpu.VMEM((2, 8, 8, FACES), F32),
            pltpu.VMEM((256, 128), F32),
            pltpu.VMEM((256, FACES), F32),
            pltpu.VMEM((PARTNERS, 256, 256), BF16),
            pltpu.VMEM((256, PARTNERS * 256), BF16),
            pltpu.VMEM((PARTNERS, 256, FACES), F32),
            pltpu.VMEM((CH, PARTNERS, 256, FACES), F32),
            pltpu.VMEM((CH, PARTNERS * 256, 256), BF16),
            pltpu.VMEM((CH, 256, FACES), F32),
            pltpu.VMEM((256, PARTNERS * FACES), BF16),
            pltpu.VMEM((128, PARTNERS * FACES), BF16),
            pltpu.VMEM((PARTNERS, 256, FACES), BF16),
            pltpu.VMEM((PARTNERS, 128, FACES), BF16),
            pltpu.VMEM((6, 2, 8, 8, CH, FACES), F32),
            pltpu.VMEM((6, 2, 8, 8, CH, FACES), F32),
            pltpu.VMEM((6, 2, 8, 8, CH, FACES), F32),
            pltpu.SemaphoreType.DMA((6, 6)),
            pltpu.SemaphoreType.DMA((6, 6)),
            pltpu.SemaphoreType.DMA((2,)),
            pltpu.SemaphoreType.DMA((28,)),
            pltpu.SemaphoreType.DMA((28,)),
            pltpu.SemaphoreType.DMA((28,)),
        ],
        compiler_params=pltpu.CompilerParams(
            collective_id=0, has_side_effects=True, vmem_limit_bytes=60 * 1024 * 1024
        ),
        name="contact",
    )(
        surface_state.reshape(ROWS, FACES),
        direction.reshape(ROWS, FACES),
        stiffness,
        partners.T,
        contact_owner.reshape(1, BLOCKS),
        projection,
        mortar,
    )
    return result.reshape(BLOCKS, CH, FACES)


def solution(mesh):
    placed = (
        P("vol", "rep", None),
        P("vol", "rep", None),
        P("vol", None),
        P("vol", None),
        P("vol"),
        P(),
        P(),
    )
    return jax.shard_map(
        local, mesh=mesh, in_specs=placed, out_specs=P("vol", "rep", None), check_vma=False
    )
```

time: 151 us -> 129 us (0.85)
  Pallas kernels: 148 us -> 127 us
    pallas_call x1, Pallas kernels: 148 us -> 127 us  [local(): pl.pallas_call(body, out_shape=jax.ShapeDtypeStruct((ROWS, FACES), F32),...]
    unnamed x4 -> x1, local copies, waits for them, and re-layouts: 3.23 us -> 1.82 us
where the time goes in v2:
time: 129 us
  Pallas kernels  127 us (98%)
  local copies, waits for them, and re-layouts  1.82 us (1%)
    pallas_call x1, Pallas kernels, local(): pl.pallas_call(body, out_shape=jax.ShapeDtypeStruct((ROWS, FACES), F32),...  127 us

profile of v2, /device:TPU:1, one launch (start us, length us, event | category | flops | bytes accessed | tf_op | source)
XLA Modules:
  0.0 129.2 jit_solution(10433532566678692192)
XLA Ops:
  0.0 127.4 %contact.1 = f32[896,128]{1,0:T(8,128)} custom-call(f32[896,128]{1,0:T(8,128)} %bitcast.6, f32[896,128]{1,0:T(8,128)} %bitcast.7, f32[112,128]{1,0:T(8,128)} %stiff_in.1, s32[4,112]{1,0:T(4,128)} %bitcast.8, s32[1,112]{1,0:T(1,128)} %bitcast.9, f32[32,32]{1,0:T(8,128)} %proj.1, f32[4,128,128]{2,1,0:T(8,128)} %mortar_in.1), custom_call_target="tpu_custom_call" | custom-call | tf_op jit(solution)/shard_map/contact/pallas_call | solution.py:501
  127.4 1.8 %copy.9 = f32[112,8,128]{2,1,0:T(8,128)} copy(f32[112,8,128]{2,1,0:T(8,128)} %bitcast.5) | data formatting | bytes 917504

commit v3 on v2

--- a/solution.py
+++ b/solution.py
@@ -38,10 +38,12 @@
     proj,
     mortar_in,
     out,
-    gs,
-    go,
-    gd,
-    gr,
+    tb,
+    tc,
+    sp,
+    dp,
+    bk,
+    hm,
     gm,
     raw,
     orow,
@@ -50,8 +52,6 @@
     sti,
     pick,
     pick_t,
-    prj,
-    prd,
     mp,
     mq,
     ms,
@@ -60,7 +60,7 @@
     g,
     gta,
     wfs,
-    wts,
+    chg,
     uhl,
     tan,
     mm,
@@ -73,6 +73,7 @@
     x_send,
     x_recv,
     x_local,
+    d_local,
     c_send,
     c_recv,
     c_local,
@@ -83,7 +84,6 @@
     z = lax.rem(vol // 2, NZ)
     core = lax.rem(vol, 2)
     right = lax.rem(rep + 1, REPS)
-    left = lax.rem(rep + 3, REPS)
 
     def along_z(peer, cross):
         return y * 16 + peer * 2 + (1 - core if cross else core)
@@ -91,13 +91,12 @@
     def along_y(peer):
         return peer * 16 + z * 2 + core
 
-    local_s = pltpu.make_async_copy(state, gs.at[rep], x_local.at[0])
-    local_s.start()
-    local_d = pltpu.make_async_copy(move, raw.at[pl.ds(0, ROWS)], x_local.at[1])
+    local_d = pltpu.make_async_copy(move, raw.at[pl.ds(0, ROWS)], d_local)
     local_d.start()
     barrier = pltpu.get_barrier_semaphore()
-    for side in (right, left):
-        pl.semaphore_signal(barrier, inc=1, device_id=(vol, side), device_id_type=MESH)
+    for side in (1, 3, 2):
+        peer = lax.rem(rep + side, REPS)
+        pl.semaphore_signal(barrier, inc=1, device_id=(vol, peer), device_id_type=MESH)
 
     def greet(o, carry):
         for peer in (
@@ -129,35 +128,69 @@
         pick[h * 128 : (h + 1) * 128, 128:256] = chosen.astype(BF16)
         pick_t[:, h * 128 : (h + 1) * 128] = chosen.T.astype(BF16)
 
-    def x_copy(src, dst, n, index, side):
-        copy = pltpu.make_async_remote_copy(
-            src_ref=src,
-            dst_ref=dst,
-            send_sem=x_send.at[n, index],
-            recv_sem=x_recv.at[n, index],
-            device_id=(vol, side),
-            device_id_type=MESH,
-        )
+    def x_send_all(src, dst, n, base):
+        copies = []
+        for side in (1, 3, 2):
+            peer = lax.rem(rep + side, REPS)
+            copy = pltpu.make_async_remote_copy(
+                src_ref=src(peer),
+                dst_ref=dst,
+                send_sem=x_send.at[n, base + side - 1],
+                recv_sem=x_recv.at[n, base + side - 1],
+                device_id=(vol, peer),
+                device_id_type=MESH,
+            )
+            copy.start()
+            copies.append(copy)
+        return copies
+
+    def turn_start(n, own, count):
+        rows = count * CH
+        dst = tb.at[n, rep, pl.ds(0, rows)]
+
+        def quarter(peer):
+            return own.at[pl.ds(peer * rows, rows)]
+
+        copies = x_send_all(quarter, dst, n, 0)
+        copy = pltpu.make_async_copy(quarter(rep), dst, x_local.at[n, 0])
         copy.start()
-        return copy
-
-    def x_start(own, view, n):
-        return [
-            x_copy(own(0), view(rep, 0), n, 0, right),
-            x_copy(own(1), view(rep, 1), n, 1, left),
-            x_copy(own(1), view(rep, 1), n, 2, right),
-            x_copy(own(0), view(rep, 0), n, 3, left),
-        ]
-
-    def x_relay(view, n, copies):
-        copies[0].wait_recv()
-        copies.append(x_copy(view(left, 0), view(left, 0), n, 4, right))
-        copies[1].wait_recv()
-        copies.append(x_copy(view(right, 1), view(right, 1), n, 5, left))
-
-    def x_finish(copies):
-        for copy in copies[2:]:
+        return copies, copy
+
+    def turn_middle(n, run, land, count, transposed):
+        rows = count * CH
+        for copy in run[0]:
             copy.wait_recv()
+        run[1].wait()
+
+        def share(r, carry):
+            total = [jnp.zeros((count, FACES), F32) for _ in range(CH)]
+            for j in range(REPS * CH):
+                x = tb[n, j // CH, pl.ds(j % CH, count, stride=CH), :]
+                for i in range(CH):
+                    factor = proj[j, r * CH + i] if transposed else proj[r * CH + i, j]
+                    total[i] = total[i] + factor * x
+            for i in range(CH):
+                tc[n, r, pl.ds(i, count, stride=CH), :] = total[i]
+            return carry
+
+        lax.fori_loop(0, REPS, share, 0)
+        dst = land.at[pl.ds(rep * rows, rows)]
+
+        def back(peer):
+            return tc.at[n, peer, pl.ds(0, rows)]
+
+        copies = x_send_all(back, dst, n, 3)
+        copy = pltpu.make_async_copy(back(rep), dst, x_local.at[n, 1])
+        copy.start()
+        sent.extend(run[0] + copies)
+        return copies, copy
+
+    def turn_end(run):
+        for copy in run[0]:
+            copy.wait_recv()
+        run[1].wait()
+
+    sent = []
 
     def phase(dim, cross, src, dst, sem):
         mine = z if dim == "z" else y
@@ -218,6 +251,12 @@
         b = phase("z", True, lambda i: p.at[n, 1, i], lambda i: q.at[n, 1, i], 4 * n + 1)
         return a, b
 
+    def back_one_from(n, source):
+        first = source.reshape(2, 8, 8, CH, FACES)
+        a = phase("y", False, lambda i: first.at[0, i], lambda i: q.at[n, 0, i], 4 * n)
+        b = phase("z", True, lambda i: first.at[1, i], lambda i: q.at[n, 1, i], 4 * n + 1)
+        return a, b
+
     def back_two(n, run):
         drain(run[0], q.at[n, 0], 4 * n)
         a = phase("z", False, lambda i: q.at[n, 0, :, i], lambda i: o.at[n, 0, i], 4 * n + 2)
@@ -238,25 +277,8 @@
         high, low = split(x)
         return dot(rows, jnp.concatenate([high, low], axis=0))
 
-    def gs_view(origin, part):
-        return gs.at[origin, pl.ds(part * (ROWS // 2), ROWS // 2)]
-
-    def go_view(origin, part):
-        return go.at[origin, pl.ds(part * (ROWS // 2), ROWS // 2)]
-
-    def gr_view(origin, part):
-        return gr.at[origin, pl.ds(part * 64 * CH, 64 * CH)]
-
-    def gm_view(origin, part):
-        return gm.at[origin, part]
-
-    def gd_view(h):
-        return lambda origin, part: gd.at[h, part, origin]
-
-    pl.semaphore_wait(barrier, 24)
-    x_state = x_start(
-        lambda part: state.at[pl.ds(part * (ROWS // 2), ROWS // 2)], gs_view, 0
-    )
+    pl.semaphore_wait(barrier, 25)
+    turn_s = turn_start(0, state, BLOCKS // REPS)
 
     lab_t[...] = jnp.zeros((128, 128), F32)
     lab_t[0:PARTNERS, 0:BLOCKS] = (partners_in[...] + 1).astype(F32)
@@ -296,7 +318,8 @@
         phase("y", False, lambda i: ms.at[0, i], lambda i: gm.at[rep, 0, i], 26),
         phase("z", True, lambda i: ms.at[1, i], lambda i: gm.at[rep, 1, i], 27),
     )
-    x_relay(gs_view, 0, x_state)
+    sp[ROWS:, :] = jnp.zeros((128 * CH - ROWS, FACES), F32)
+    turn_s = turn_middle(0, turn_s, sp, BLOCKS // REPS, False)
 
     for k in range(PARTNERS):
         cols = slice(k * FACES, (k + 1) * FACES)
@@ -308,48 +331,32 @@
         mth[k, 0:FACES, :] = high
         mth[k, FACES : 2 * FACES, :] = high
         mtl[k] = low
-    prj[...] = jnp.zeros((CH, 128, FACES), F32)
-
-    def land_d(h):
-        return lambda part: gd.at[h, part, rep]
-
-    runs[0] = there_two(0, runs[0], land_d(0))
+
+    def land(n):
+        return lambda part: o.at[n, part]
+
+    def slots(n):
+        return o.at[n].reshape(SLOTS * CH, FACES)
+
+    runs[0] = there_two(0, runs[0], land(0))
     drain(meta[0], gm.at[rep, 0], 26)
     drain(meta[1], gm.at[rep, 1], 27)
-    x_meta = x_start(lambda part: gm.at[rep, part], gm_view, 1)
-    runs[1] = there_two(1, runs[1], land_d(1))
-    there_end(0, runs[0], land_d(0))
-    x_d0 = x_start(lambda part: gd.at[0, part, rep], gd_view(0), 2)
-
-    def project(load, count, transposed, base):
-        total = [jnp.zeros((count, FACES), F32) for _ in range(4)]
-        for j in range(REPS * CH):
-            x = load(j)
-            for i in range(4):
-                if transposed:
-                    factor = proj[j, rep * CH + base + i]
-                else:
-                    factor = proj[rep * CH + base + i, j]
-                total[i] = total[i] + factor * x
-        return total
-
-    def rows_of(ref, start):
-        return lambda j: ref[j // CH, pl.ds(start * CH + j % CH, 56, stride=CH), :]
-
-    x_finish(x_state)
-    local_s.wait()
-    for start in (0, 56):
-        for base in (0, 4):
-            total = project(rows_of(gs, start), 56, False, base)
-            for i in range(4):
-                prj[base + i, start : start + 56, :] = total[i]
+    x_meta = x_send_all(lambda peer: gm.at[rep], gm.at[rep], 1, 0)
+    sent.extend(x_meta)
+    runs[1] = there_two(1, runs[1], land(1))
+    turn_end(turn_s)
     for h in range(2):
         for i in range(CH):
-            put(2 + h, i, chosen_rows(pick[h * 128 : (h + 1) * 128, :], prj[i]))
+            x = sp[pl.ds(i, 128, stride=CH), :]
+            put(2 + h, i, chosen_rows(pick[h * 128 : (h + 1) * 128, :], x))
         runs.append(there_one(2 + h))
-
-    x_relay(gm_view, 1, x_meta)
-    x_finish(x_meta)
+    there_end(0, runs[0], land(0))
+    turn_0 = turn_start(2, slots(0), SLOTS // REPS)
+    there_end(1, runs[1], land(1))
+    turn_1 = turn_start(3, slots(1), SLOTS // REPS)
+
+    for copy in x_meta:
+        copy.wait_recv()
     for h in range(2):
         stis[h * 128 : (h + 1) * 128] = gm.at[2 * h].reshape(128, FACES)[...]
         labs[h * 128 : (h + 1) * 128] = gm.at[2 * h + 1].reshape(128, FACES)[...]
@@ -363,32 +370,13 @@
         gta[:, k * 256 : (k + 1) * 256] = jnp.where(hit, 1.0, 0.0).astype(BF16)
         wfs[k] = dot(g[k], ones) * stis[...] * SHARPNESS
 
-    x_relay(gd_view(0), 2, x_d0)
-    there_end(1, runs[1], land_d(1))
-    x_d1 = x_start(lambda part: gd.at[1, part, rep], gd_view(1), 3)
-
-    def land(n):
-        return lambda part: o.at[n, part]
-
+    def dp_half(h):
+        return dp.at[pl.ds(h * SLOTS * CH, SLOTS * CH)]
+
+    turn_0 = turn_middle(2, turn_0, dp_half(0), SLOTS // REPS, False)
     runs[2] = there_two(2, runs[2], land(2))
-
-    def project_slots(h):
-        for part in range(2):
-
-            def load(j):
-                flat = gd.at[h, part, j // CH].reshape(64 * CH, FACES)
-                return flat[pl.ds(j % CH, 64, stride=CH), :]
-
-            for base in (0, 4):
-                total = project(load, 64, False, base)
-                start = h * 128 + part * 64
-                for i in range(4):
-                    prd[base + i, start : start + 64, :] = total[i]
-
-    x_finish(x_d0)
-    project_slots(0)
+    turn_1 = turn_middle(3, turn_1, dp_half(1), SLOTS // REPS, False)
     runs[3] = there_two(3, runs[3], land(3))
-    x_relay(gd_view(1), 3, x_d1)
 
     def mapped(x):
         high, low = split(x)
@@ -400,7 +388,13 @@
             result.append(both[:, 0:FACES] + both[:, FACES:])
         return result
 
-    def weigh(i, carry):
+    def change(i, carry):
+        x = dp[pl.ds(i, 256, stride=CH), :]
+        for k, partner in enumerate(mapped(x)):
+            chg[i, k] = x - partner
+        return carry
+
+    def pull(i, carry):
         x = jnp.concatenate(
             [
                 o.at[2 + h, part].reshape(64 * CH, FACES)[pl.ds(i, 64, stride=CH), :]
@@ -409,22 +403,10 @@
             ],
             axis=0,
         )
+        total = jnp.zeros((256, FACES), F32)
         for k, partner in enumerate(mapped(x)):
             squashed = 1.0 / (1.0 + jnp.exp(-SHARPNESS * (x - partner)))
-            wts[i, k] = wfs[k] * squashed * (1.0 - squashed)
-        return carry
-
-    there_end(2, runs[2], land(2))
-    there_end(3, runs[3], land(3))
-    lax.fori_loop(0, CH, weigh, 0)
-    x_finish(x_d1)
-    project_slots(1)
-
-    def pull(i, carry):
-        x = prd[i]
-        total = jnp.zeros((256, FACES), F32)
-        for k, partner in enumerate(mapped(x)):
-            traction = wts[i, k] * (x - partner)
+            traction = wfs[k] * squashed * (1.0 - squashed) * chg[i, k]
             total = total + traction
             high, low = split(traction)
             pulled = dot(jnp.concatenate([high, low], axis=1), mth[k]) + dot(high, mtl[k])
@@ -437,28 +419,22 @@
         both = dot(gta[h * 128 : (h + 1) * 128, :], uhl[i])
         return tan[i, h * 128 : (h + 1) * 128, :] - both[:, 0:FACES] - both[:, FACES:]
 
+    turn_end(turn_0)
+    turn_end(turn_1)
+    lax.fori_loop(0, CH, change, 0)
+    there_end(2, runs[2], land(2))
+    there_end(3, runs[3], land(3))
     lax.fori_loop(0, CH, pull, 0)
-    mine = gr.at[rep]
     for i in range(CH):
-        mine[pl.ds(i, 128, stride=CH), :] = summed(i, 1)
-    x_back = x_start(lambda part: gr_view(rep, part), gr_view, 4)
+        bk[0, pl.ds(i, 128, stride=CH), :] = summed(i, 1)
+    turn_b = turn_start(4, bk.at[0], SLOTS // REPS)
     for i in range(CH):
         put(4, i, summed(i, 0))
     run_first = back_one(4)
-    x_relay(gr_view, 4, x_back)
+    run_second = turn_middle(4, turn_b, bk.at[1], SLOTS // REPS, True)
     run_first = back_two(4, run_first)
-    x_finish(x_back)
-    for part in range(2):
-
-        def load(j):
-            return gr[j // CH, pl.ds(part * 64 * CH + j % CH, 64, stride=CH), :]
-
-        dst = p.at[5, part].reshape(64 * CH, FACES)
-        for base in (0, 4):
-            total = project(load, 64, True, base)
-            for i in range(4):
-                dst[pl.ds(base + i, 64, stride=CH), :] = total[i]
-    run_second = back_one(5)
+    turn_end(run_second)
+    run_second = back_one_from(5, bk.at[1])
     back_end(4, run_first)
 
     def home(n, i):
@@ -474,24 +450,17 @@
         both = dot(pick_t[:, h * 128 : (h + 1) * 128], jnp.concatenate([high, low], axis=1))
         return (both[:, 0:FACES] + both[:, FACES:])[0:BLOCKS]
 
-    mine = go.at[rep]
     for i in range(CH):
-        mine[pl.ds(i, BLOCKS, stride=CH), :] = home(4, i)
-    x_home = x_start(lambda part: go_view(rep, part), go_view, 5)
+        hm[0, pl.ds(i, BLOCKS, stride=CH), :] = home(4, i)
+    turn_h = turn_start(5, hm.at[0], BLOCKS // REPS)
     run_second = back_two(5, run_second)
-    x_relay(go_view, 5, x_home)
+    turn_h = turn_middle(5, turn_h, hm.at[1], BLOCKS // REPS, True)
     back_end(5, run_second)
+    late = [home(5, i) for i in range(CH)]
+    turn_end(turn_h)
     for i in range(CH):
-        prj[i, 0:BLOCKS, :] = home(5, i)
-    x_finish(x_home)
-    for start in (0, 56):
-        for base in (0, 4):
-            total = project(rows_of(go, start), 56, True, base)
-            for i in range(4):
-                out[pl.ds(start * CH + base + i, 56, stride=CH), :] = (
-                    total[i] + prj[base + i, start : start + 56, :]
-                )
-    for copy in x_state + x_meta + x_d0 + x_d1 + x_back + x_home:
+        out[pl.ds(i, BLOCKS, stride=CH), :] = hm[1, pl.ds(i, BLOCKS, stride=CH), :] + late[i]
+    for copy in sent:
         copy.wait_send()
 
 
@@ -512,10 +481,12 @@
         ],
         out_specs=vmem,
         scratch_shapes=[
-            pltpu.VMEM((REPS, ROWS, FACES), F32),
-            pltpu.VMEM((REPS, ROWS, FACES), F32),
-            pltpu.VMEM((2, 2, REPS, 8, 8, CH, FACES), F32),
-            pltpu.VMEM((REPS, SLOTS * CH, FACES), F32),
+            pltpu.VMEM((6, REPS, 32 * CH, FACES), F32),
+            pltpu.VMEM((6, REPS, 32 * CH, FACES), F32),
+            pltpu.VMEM((128 * CH, FACES), F32),
+            pltpu.VMEM((2 * SLOTS * CH, FACES), F32),
+            pltpu.VMEM((2, SLOTS * CH, FACES), F32),
+            pltpu.VMEM((2, ROWS, FACES), F32),
             pltpu.VMEM((REPS, 2, 8, 8, FACES), F32),
             pltpu.VMEM((128 * CH, FACES), F32),
             pltpu.VMEM((8, 128), F32),
@@ -524,8 +495,6 @@
             pltpu.VMEM((128, FACES), F32),
             pltpu.VMEM((256, 256), BF16),
             pltpu.VMEM((128, 256), BF16),
-            pltpu.VMEM((CH, 128, FACES), F32),
-            pltpu.VMEM((CH, 256, FACES), F32),
             pltpu.VMEM((2, 8, 8, FACES), F32),
             pltpu.VMEM((2, 8, 8, FACES), F32),
             pltpu.VMEM((2, 8, 8, FACES), F32),
@@ -546,7 +515,8 @@
             pltpu.VMEM((6, 2, 8, 8, CH, FACES), F32),
             pltpu.SemaphoreType.DMA((6, 6)),
             pltpu.SemaphoreType.DMA((6, 6)),
-            pltpu.SemaphoreType.DMA((2,)),
+            pltpu.SemaphoreType.DMA((6, 2)),
+            pltpu.SemaphoreType.DMA,
             pltpu.SemaphoreType.DMA((28,)),
             pltpu.SemaphoreType.DMA((28,)),
             pltpu.SemaphoreType.DMA((28,)),

time: 129 us -> 114 us (0.88)
  Pallas kernels: 127 us -> 112 us
    pallas_call x1, Pallas kernels: 127 us -> 112 us  [local(): pl.pallas_call(body, out_shape=jax.ShapeDtypeStruct((ROWS, FACES), F32),...]
where the time goes in v3:
time: 114 us
  Pallas kernels  112 us (98%)
  local copies, waits for them, and re-layouts  1.82 us (2%)
    pallas_call x1, Pallas kernels, local(): pl.pallas_call(body, out_shape=jax.ShapeDtypeStruct((ROWS, FACES), F32),...  112 us

profile of v3, /device:TPU:1, one launch (start us, length us, event | category | flops | bytes accessed | tf_op | source)
XLA Modules:
  0.0 114.1 jit_solution(1733008646062502740)
XLA Ops:
  0.0 112.3 %contact.1 = f32[896,128]{1,0:T(8,128)} custom-call(f32[896,128]{1,0:T(8,128)} %bitcast.6, f32[896,128]{1,0:T(8,128)} %bitcast.7, f32[112,128]{1,0:T(8,128)} %stiff_in.1, s32[4,112]{1,0:T(4,128)} %bitcast.8, s32[1,112]{1,0:T(1,128)} %bitcast.9, f32[32,32]{1,0:T(8,128)} %proj.1, f32[4,128,128]{2,1,0:T(8,128)} %mortar_in.1), custom_call_target="tpu_custom_call" | custom-call | tf_op jit(solution)/shard_map/contact/pallas_call | solution.py:470
  112.3 1.8 %copy.9 = f32[112,8,128]{2,1,0:T(8,128)} copy(f32[112,8,128]{2,1,0:T(8,128)} %bitcast.5) | data formatting | bytes 917504

commit v4 on v3

--- a/solution.py
+++ b/solution.py
@@ -117,10 +117,19 @@
     across = jnp.broadcast_to(orow[0:1, :], (128, 128))
     down = across.T
     rank = jnp.sum(jnp.where((across == down) & (row < lane), 1.0, 0.0), axis=0, keepdims=True)
-    major = lax.rem(row // 8, 8)
-    minor = lax.rem(row, 8)
+    parity = row // 64
+    part_b = lax.rem(row // 32, 2)
+    major = lax.rem(row // 4, 8)
+    minor = 2 * lax.rem(row, 4) + lax.rem(y + z + major + parity, 2)
     dest = jnp.where(
-        row < 64, minor * 16 + major * 2 + core, major * 16 + minor * 2 + (1 - core)
+        part_b == 0, minor * 16 + major * 2 + core, major * 16 + minor * 2 + (1 - core)
+    ).astype(F32)
+    plain_major = lax.rem(row // 8, 8)
+    plain_minor = lax.rem(row, 8)
+    plain = jnp.where(
+        row < 64,
+        plain_minor * 16 + plain_major * 2 + core,
+        plain_major * 16 + plain_minor * 2 + (1 - core),
     ).astype(F32)
     for h in range(2):
         chosen = jnp.where((across == dest) & (rank == float(h)), 1.0, 0.0)
@@ -230,55 +239,53 @@
         whole.wait_recv()
         whole.wait_send()
 
-    def there_one(n):
-        a = phase("z", False, lambda i: p.at[n, 0, i], lambda i: q.at[n, 0, i], 4 * n)
-        b = phase("y", False, lambda i: p.at[n, 1, i], lambda i: q.at[n, 1, i], 4 * n + 1)
-        return a, b
-
-    def there_two(n, run, land):
-        drain(run[0], q.at[n, 0], 4 * n)
-        a = phase("y", False, lambda i: q.at[n, 0, :, i], lambda i: land(0).at[i], 4 * n + 2)
-        drain(run[1], q.at[n, 1], 4 * n + 1)
-        b = phase("z", True, lambda i: q.at[n, 1, :, i], lambda i: land(1).at[i], 4 * n + 3)
-        return a, b
-
-    def there_end(n, run, land):
-        drain(run[0], land(0), 4 * n + 2)
-        drain(run[1], land(1), 4 * n + 3)
-
-    def back_one(n):
-        a = phase("y", False, lambda i: p.at[n, 0, i], lambda i: q.at[n, 0, i], 4 * n)
-        b = phase("z", True, lambda i: p.at[n, 1, i], lambda i: q.at[n, 1, i], 4 * n + 1)
-        return a, b
-
-    def back_one_from(n, source):
-        first = source.reshape(2, 8, 8, CH, FACES)
-        a = phase("y", False, lambda i: first.at[0, i], lambda i: q.at[n, 0, i], 4 * n)
-        b = phase("z", True, lambda i: first.at[1, i], lambda i: q.at[n, 1, i], 4 * n + 1)
-        return a, b
-
-    def back_two(n, run):
-        drain(run[0], q.at[n, 0], 4 * n)
-        a = phase("z", False, lambda i: q.at[n, 0, :, i], lambda i: o.at[n, 0, i], 4 * n + 2)
-        drain(run[1], q.at[n, 1], 4 * n + 1)
-        b = phase("y", False, lambda i: q.at[n, 1, :, i], lambda i: o.at[n, 1, i], 4 * n + 3)
-        return a, b
-
-    def back_end(n, run):
-        drain(run[0], o.at[n, 0], 4 * n + 2)
-        drain(run[1], o.at[n, 1], 4 * n + 3)
+    def one(n, s, part, dim, cross, source):
+        return phase(
+            dim,
+            cross,
+            lambda i: source.at[s, part, i],
+            lambda i: q.at[n, s, part, i // 2, lax.rem(i, 2)],
+            8 * n + 4 * s + part,
+        )
+
+    def two(n, s, part, dim, cross):
+        return phase(
+            dim,
+            cross,
+            lambda i: q.at[n, s, part, :, lax.rem(i + y + z + s, 2), i // 2],
+            lambda i: o.at[n, s, part, i],
+            8 * n + 4 * s + 2 + part,
+        )
+
+    def there_one(n, s):
+        source = p.at[n]
+        return one(n, s, 0, "z", False, source), one(n, s, 1, "y", False, source)
+
+    def there_two(n, s, run):
+        drain(run[0], p.at[n, s, 0], 8 * n + 4 * s)
+        a = two(n, s, 0, "y", False)
+        drain(run[1], p.at[n, s, 1], 8 * n + 4 * s + 1)
+        return a, two(n, s, 1, "z", True)
+
+    def back_one(n, s, source):
+        return one(n, s, 0, "y", False, source), one(n, s, 1, "z", True, source)
+
+    def back_two(n, s, run):
+        drain(run[0], p.at[n, s, 0], 8 * n + 4 * s)
+        a = two(n, s, 0, "z", False)
+        drain(run[1], p.at[n, s, 1], 8 * n + 4 * s + 1)
+        return a, two(n, s, 1, "y", False)
+
+    def end(n, s, run):
+        for part in range(2):
+            drain(run[part], o.at[n, s, part], 8 * n + 4 * s + 2 + part)
 
     def put(n, i, rows):
-        for part in range(2):
-            dst = p.at[n, part].reshape(64 * CH, FACES)
-            dst[pl.ds(i, 64, stride=CH), :] = rows[part * 64 : (part + 1) * 64]
+        p.at[n].reshape(SLOTS * CH, FACES)[pl.ds(i, SLOTS, stride=CH), :] = rows
 
     def chosen_rows(rows, x):
         high, low = split(x)
         return dot(rows, jnp.concatenate([high, low], axis=0))
-
-    pl.semaphore_wait(barrier, 25)
-    turn_s = turn_start(0, state, BLOCKS // REPS)
 
     lab_t[...] = jnp.zeros((128, 128), F32)
     lab_t[0:PARTNERS, 0:BLOCKS] = (partners_in[...] + 1).astype(F32)
@@ -290,33 +297,37 @@
     sti[...] = jnp.zeros((128, FACES), F32)
     sti[0:BLOCKS, :] = stiff_in[...]
     table = jnp.where(lax.rem(rep, 2) == 0, sti[...], lab[...])
-    rows = chosen_rows(pick[pl.ds((rep // 2) * 128, 128), :], table)
+    plain_rank = (rep // 2).astype(F32)
+    chosen = jnp.where((across == plain) & (rank == plain_rank), 1.0, 0.0).astype(BF16)
+    rows = chosen_rows(jnp.concatenate([chosen, chosen], axis=1), table)
     for part in range(2):
         for i in range(8):
             mp[part, i] = rows[part * 64 + i * 8 : part * 64 + (i + 1) * 8]
-    meta = (
-        phase("z", False, lambda i: mp.at[0, i], lambda i: mq.at[0, i], 24),
-        phase("y", False, lambda i: mp.at[1, i], lambda i: mq.at[1, i], 25),
-    )
-
     raw[ROWS:, :] = jnp.zeros((128 * CH - ROWS, FACES), F32)
     local_d.wait()
-    runs = []
     for h in range(2):
         for i in range(CH):
             x = raw[pl.ds(i, 128, stride=CH), :]
             put(h, i, chosen_rows(pick[h * 128 : (h + 1) * 128, :], x))
-        runs.append(there_one(h))
-
-    drain(meta[0], mq.at[0], 24)
-    drain(meta[1], mq.at[1], 25)
+
+    pl.semaphore_wait(barrier, 25)
+    turn_s = turn_start(0, state, BLOCKS // REPS)
+
+    meta = (
+        phase("z", False, lambda i: mp.at[0, i], lambda i: mq.at[0, i], 48),
+        phase("y", False, lambda i: mp.at[1, i], lambda i: mq.at[1, i], 49),
+    )
+    runs = [[there_one(n, s) for s in range(2)] for n in range(2)]
+
+    drain(meta[0], mq.at[0], 48)
+    drain(meta[1], mq.at[1], 49)
     for part in range(2):
         flat = mq.at[part].reshape(64, FACES)
         for i in range(8):
             ms[part, i] = flat[pl.ds(i, 8, stride=8), :]
     meta = (
-        phase("y", False, lambda i: ms.at[0, i], lambda i: gm.at[rep, 0, i], 26),
-        phase("z", True, lambda i: ms.at[1, i], lambda i: gm.at[rep, 1, i], 27),
+        phase("y", False, lambda i: ms.at[0, i], lambda i: gm.at[rep, 0, i], 50),
+        phase("z", True, lambda i: ms.at[1, i], lambda i: gm.at[rep, 1, i], 51),
     )
     sp[ROWS:, :] = jnp.zeros((128 * CH - ROWS, FACES), F32)
     turn_s = turn_middle(0, turn_s, sp, BLOCKS // REPS, False)
@@ -332,34 +343,39 @@
         mth[k, FACES : 2 * FACES, :] = high
         mtl[k] = low
 
-    def land(n):
-        return lambda part: o.at[n, part]
-
     def slots(n):
         return o.at[n].reshape(SLOTS * CH, FACES)
 
-    runs[0] = there_two(0, runs[0], land(0))
-    drain(meta[0], gm.at[rep, 0], 26)
-    drain(meta[1], gm.at[rep, 1], 27)
+    runs[0] = [there_two(0, s, runs[0][s]) for s in range(2)]
+    drain(meta[0], gm.at[rep, 0], 50)
+    drain(meta[1], gm.at[rep, 1], 51)
     x_meta = x_send_all(lambda peer: gm.at[rep], gm.at[rep], 1, 0)
     sent.extend(x_meta)
-    runs[1] = there_two(1, runs[1], land(1))
+    runs[1] = [there_two(1, s, runs[1][s]) for s in range(2)]
     turn_end(turn_s)
     for h in range(2):
         for i in range(CH):
             x = sp[pl.ds(i, 128, stride=CH), :]
             put(2 + h, i, chosen_rows(pick[h * 128 : (h + 1) * 128, :], x))
-        runs.append(there_one(2 + h))
-    there_end(0, runs[0], land(0))
+        runs.append([there_one(2 + h, s) for s in range(2)])
+    for s in range(2):
+        end(0, s, runs[0][s])
     turn_0 = turn_start(2, slots(0), SLOTS // REPS)
-    there_end(1, runs[1], land(1))
+    for s in range(2):
+        end(1, s, runs[1][s])
     turn_1 = turn_start(3, slots(1), SLOTS // REPS)
 
     for copy in x_meta:
         copy.wait_recv()
+    turn_rows = jnp.where(lane == part_b * 64 + major * 8 + minor, 1.0, 0.0).astype(BF16)
+    turn_rows = jnp.concatenate([turn_rows, turn_rows], axis=1)
     for h in range(2):
-        stis[h * 128 : (h + 1) * 128] = gm.at[2 * h].reshape(128, FACES)[...]
-        labs[h * 128 : (h + 1) * 128] = gm.at[2 * h + 1].reshape(128, FACES)[...]
+        stis[h * 128 : (h + 1) * 128] = chosen_rows(
+            turn_rows, gm.at[2 * h].reshape(128, FACES)[...]
+        )
+        labs[h * 128 : (h + 1) * 128] = chosen_rows(
+            turn_rows, gm.at[2 * h + 1].reshape(128, FACES)[...]
+        )
     labels = labs[...]
     turned = labels.T
     ones = jnp.ones((256, FACES), BF16)
@@ -374,9 +390,9 @@
         return dp.at[pl.ds(h * SLOTS * CH, SLOTS * CH)]
 
     turn_0 = turn_middle(2, turn_0, dp_half(0), SLOTS // REPS, False)
-    runs[2] = there_two(2, runs[2], land(2))
+    runs[2] = [there_two(2, s, runs[2][s]) for s in range(2)]
     turn_1 = turn_middle(3, turn_1, dp_half(1), SLOTS // REPS, False)
-    runs[3] = there_two(3, runs[3], land(3))
+    runs[3] = [there_two(3, s, runs[3][s]) for s in range(2)]
 
     def mapped(x):
         high, low = split(x)
@@ -396,11 +412,7 @@
 
     def pull(i, carry):
         x = jnp.concatenate(
-            [
-                o.at[2 + h, part].reshape(64 * CH, FACES)[pl.ds(i, 64, stride=CH), :]
-                for h in range(2)
-                for part in range(2)
-            ],
+            [slots(2 + h)[pl.ds(i, SLOTS, stride=CH), :] for h in range(2)],
             axis=0,
         )
         total = jnp.zeros((256, FACES), F32)
@@ -422,42 +434,52 @@
     turn_end(turn_0)
     turn_end(turn_1)
     lax.fori_loop(0, CH, change, 0)
-    there_end(2, runs[2], land(2))
-    there_end(3, runs[3], land(3))
+    for h in range(2, 4):
+        for s in range(2):
+            end(h, s, runs[h][s])
     lax.fori_loop(0, CH, pull, 0)
     for i in range(CH):
         bk[0, pl.ds(i, 128, stride=CH), :] = summed(i, 1)
-    turn_b = turn_start(4, bk.at[0], SLOTS // REPS)
+    part_rows = SLOTS * CH // 2
+
+    def bk_half(k, s):
+        return bk.at[k, pl.ds(s * part_rows, part_rows)]
+
+    turn_b = [turn_start(4 + s, bk_half(0, s), SLOTS // REPS // 2) for s in range(2)]
     for i in range(CH):
         put(4, i, summed(i, 0))
-    run_first = back_one(4)
-    run_second = turn_middle(4, turn_b, bk.at[1], SLOTS // REPS, True)
-    run_first = back_two(4, run_first)
-    turn_end(run_second)
-    run_second = back_one_from(5, bk.at[1])
-    back_end(4, run_first)
+    first = [back_one(4, s, p.at[4]) for s in range(2)]
+    for s in range(2):
+        turn_b[s] = turn_middle(4 + s, turn_b[s], bk_half(1, s), SLOTS // REPS // 2, True)
+        first[s] = back_two(4, s, first[s])
+    second = []
+    for s in range(2):
+        turn_end(turn_b[s])
+        second.append(back_one(5, s, bk.at[1].reshape(2, 2, 8, 4, CH, FACES)))
+    for s in range(2):
+        end(4, s, first[s])
 
     def home(n, i):
-        x = jnp.concatenate(
-            [
-                o.at[n, part].reshape(64 * CH, FACES)[pl.ds(i, 64, stride=CH), :]
-                for part in range(2)
-            ],
-            axis=0,
-        )
-        high, low = split(x)
+        high, low = split(slots(n)[pl.ds(i, SLOTS, stride=CH), :])
         h = n - 4
         both = dot(pick_t[:, h * 128 : (h + 1) * 128], jnp.concatenate([high, low], axis=1))
         return (both[:, 0:FACES] + both[:, FACES:])[0:BLOCKS]
 
+    def hm_half(k, s):
+        return hm.at[k, pl.ds(s * (ROWS // 2), ROWS // 2)]
+
     for i in range(CH):
         hm[0, pl.ds(i, BLOCKS, stride=CH), :] = home(4, i)
-    turn_h = turn_start(5, hm.at[0], BLOCKS // REPS)
-    run_second = back_two(5, run_second)
-    turn_h = turn_middle(5, turn_h, hm.at[1], BLOCKS // REPS, True)
-    back_end(5, run_second)
+    turn_h = [turn_start(6 + s, hm_half(0, s), BLOCKS // REPS // 2) for s in range(2)]
+    for s in range(2):
+        second[s] = back_two(5, s, second[s])
+    for s in range(2):
+        turn_h[s] = turn_middle(6 + s, turn_h[s], hm_half(1, s), BLOCKS // REPS // 2, True)
+    for s in range(2):
+        end(5, s, second[s])
     late = [home(5, i) for i in range(CH)]
-    turn_end(turn_h)
+    for s in range(2):
+        turn_end(turn_h[s])
     for i in range(CH):
         out[pl.ds(i, BLOCKS, stride=CH), :] = hm[1, pl.ds(i, BLOCKS, stride=CH), :] + late[i]
     for copy in sent:
@@ -481,8 +503,8 @@
         ],
         out_specs=vmem,
         scratch_shapes=[
-            pltpu.VMEM((6, REPS, 32 * CH, FACES), F32),
-            pltpu.VMEM((6, REPS, 32 * CH, FACES), F32),
+            pltpu.VMEM((8, REPS, 32 * CH, FACES), F32),
+            pltpu.VMEM((8, REPS, 32 * CH, FACES), F32),
             pltpu.VMEM((128 * CH, FACES), F32),
             pltpu.VMEM((2 * SLOTS * CH, FACES), F32),
             pltpu.VMEM((2, SLOTS * CH, FACES), F32),
@@ -510,16 +532,16 @@
             pltpu.VMEM((128, PARTNERS * FACES), BF16),
             pltpu.VMEM((PARTNERS, 256, FACES), BF16),
             pltpu.VMEM((PARTNERS, 128, FACES), BF16),
-            pltpu.VMEM((6, 2, 8, 8, CH, FACES), F32),
-            pltpu.VMEM((6, 2, 8, 8, CH, FACES), F32),
-            pltpu.VMEM((6, 2, 8, 8, CH, FACES), F32),
-            pltpu.SemaphoreType.DMA((6, 6)),
-            pltpu.SemaphoreType.DMA((6, 6)),
-            pltpu.SemaphoreType.DMA((6, 2)),
+            pltpu.VMEM((6, 2, 2, 8, 4, CH, FACES), F32),
+            pltpu.VMEM((6, 2, 2, 4, 2, 4, CH, FACES), F32),
+            pltpu.VMEM((6, 2, 2, 8, 4, CH, FACES), F32),
+            pltpu.SemaphoreType.DMA((8, 6)),
+            pltpu.SemaphoreType.DMA((8, 6)),
+            pltpu.SemaphoreType.DMA((8, 2)),
             pltpu.SemaphoreType.DMA,
-            pltpu.SemaphoreType.DMA((28,)),
-            pltpu.SemaphoreType.DMA((28,)),
-            pltpu.SemaphoreType.DMA((28,)),
+            pltpu.SemaphoreType.DMA((52,)),
+            pltpu.SemaphoreType.DMA((52,)),
+            pltpu.SemaphoreType.DMA((52,)),
         ],
         compiler_params=pltpu.CompilerParams(
             collective_id=0, has_side_effects=True, vmem_limit_bytes=60 * 1024 * 1024

time: 114 us -> 112 us (0.982); the launches traced: 114 us -> 111 us
  Pallas kernels: 112 us -> 109 us
    pallas_call x1, Pallas kernels: 112 us -> 109 us  [local(): pl.pallas_call(body, out_shape=jax.ShapeDtypeStruct((ROWS, FACES), F32),...]
where the time goes in v4:
time: 112 us; the launch traced here: 111 us
  Pallas kernels  109 us (97%)
  local copies, waits for them, and re-layouts  1.82 us (2%)
    pallas_call x1, Pallas kernels, local(): pl.pallas_call(body, out_shape=jax.ShapeDtypeStruct((ROWS, FACES), F32),...  109 us

profile of v4, /device:TPU:1, one launch (start us, length us, event | category | flops | bytes accessed | tf_op | source)
XLA Modules:
  0.0 110.9 jit_solution(365814219426930950)
XLA Ops:
  0.0 109.1 %contact.1 = f32[896,128]{1,0:T(8,128)} custom-call(f32[896,128]{1,0:T(8,128)} %bitcast.6, f32[896,128]{1,0:T(8,128)} %bitcast.7, f32[112,128]{1,0:T(8,128)} %stiff_in.1, s32[4,112]{1,0:T(4,128)} %bitcast.8, s32[1,112]{1,0:T(1,128)} %bitcast.9, f32[32,32]{1,0:T(8,128)} %proj.1, f32[4,128,128]{2,1,0:T(8,128)} %mortar_in.1), custom_call_target="tpu_custom_call" | custom-call | tf_op jit(solution)/shard_map/contact/pallas_call | solution.py:492
  109.1 1.8 %copy.9 = f32[112,8,128]{2,1,0:T(8,128)} copy(f32[112,8,128]{2,1,0:T(8,128)} %bitcast.5) | data formatting | bytes 917504
